TPU v7x, 512 devices: a whole 4x4x16 slice. The times are simulated.
512 devices in a mesh: wide: 64 (over x, z), narrow: 8 (over y, core).
Axes of the slice: x: 4, y: 4, z: 16, core: 2. Of those that a mesh axis runs over, the one named last changes fastest.
Arguments:
- residual: bfloat16 [256, 16384], P('narrow', 'wide'), may hold values from -54 to 54
- norm_gain: bfloat16 [16384], P('wide'), may hold values from 0.5 to 1.5
- w_query: bfloat16 [16384, 16384], P('wide', 'narrow'), may hold values from -0.046875 to 0.046875
- w_keyval: bfloat16 [16384, 2, 1024], P('wide', None, 'narrow'), may hold values from -0.046875 to 0.046875
- w_out: bfloat16 [16384, 16384], P('narrow', 'wide'), may hold values from -0.375 to 0.375
- cache_rows: bfloat16 [256, 768, 2, 1024], P('wide', None, None, 'narrow'), may hold values from -106 to 106, as said below
- lengths: int32 [256], replicated, may hold values from 1 to 768, 49152 in all
- assignment: int32 [256], replicated, may hold values from 0 to 255, each once
Outputs:
- layer_out: bfloat16 [256, 16384], P('narrow', 'wide')
Inputs may be any that keep to these rules, and one draw needn't show every extreme that they name: `lengths`: largest entry reaches 768. `assignment`: each row named once. `cache_rows`: entries at positions at or beyond a row's length are not read.
All inputs are finite; a program needn't handle non-finite values.
Results may differ from a plain program's by a relative error of at most 0.012.
The roundings to bfloat16 on the way count: a program that leaves them out, or rounds other values in their place, can miss the bound.
Values may be sent and summed in bfloat16 or wider, within the bound.
A program may use at most 64 MiB of HBM per device.

v0:
```python
import math

import jax
import jax.numpy as jnp
from jax import lax
from jax.sharding import Mesh
from jax.sharding import PartitionSpec as P

D = 16384
HD = 128
WIDE = ("wide_0", "wide_1")


def copy_for_each(shard, axis):
    copies = jnp.broadcast_to(shard, (lax.axis_size(axis), *shard.shape))
    return lax.all_to_all(copies, axis, split_axis=0, concat_axis=0, tiled=True)


def joined_along(tiles, dim):
    lengths = list(tiles.shape[1:])
    lengths[dim] *= tiles.shape[0]
    return jnp.moveaxis(tiles, 0, dim).reshape(lengths)


def collect(shard, axis, dim):
    tiles = copy_for_each(shard, axis)
    return joined_along(tiles, dim)


def by_axis(shard, axes):
    for axis in axes:
        shard = lax.psum(shard, axis)
    return shard


def cut_along(shard, dim, count):
    lengths = shard.shape
    tiles = shard.reshape(*lengths[:dim], count, lengths[dim] // count, *lengths[dim + 1 :])
    return jnp.moveaxis(tiles, dim, 0)


def sum_at_owner(shard, axis, dim):
    tiles = cut_along(shard, dim, lax.axis_size(axis))
    arrived = lax.all_to_all(tiles, axis, split_axis=0, concat_axis=0, tiled=True)
    return arrived.sum(axis=0)


def sum_by_axis(shard, axes, dim):
    far, near = axes
    initial = sum_at_owner(shard, far, dim)
    return sum_at_owner(initial, near, dim)


def gather_in_order(shard, axes, turns):
    tiles = shard[None]
    for k in turns:
        tiles = lax.all_gather(tiles, axes[k], axis=0, tiled=True)
    carried = [lax.axis_size(axes[k]) for k in reversed(turns)]
    tiles = tiles.reshape(*carried, *shard.shape)
    turned = sorted(range(len(turns)), key=lambda place: turns[len(turns) - 1 - place])
    return tiles.transpose(*turned, *range(len(turns), tiles.ndim)).reshape(-1, *shard.shape)


def whole_of(shard, axes, turns, dim):
    return joined_along(gather_in_order(shard, axes, turns), dim)


def rotate(values, positions):
    half_dim = values.shape[-1] // 2
    freqs = 500000.0 ** (-(jnp.arange(half_dim, dtype=jnp.float32) * 2.0 / values.shape[-1]))
    angles = positions[..., None] * freqs
    cosine = jnp.cos(angles)
    sine = jnp.sin(angles)
    first_half = values[..., :half_dim]
    second_half = values[..., half_dim:]
    return jnp.concatenate(
        [first_half * cosine - second_half * sine, second_half * cosine + first_half * sine],
        axis=-1,
    )


def attend(queries, keys_new, values_new, cache_rows, slot_lengths, block_count, block_len):
    slot_count, groups_local, group_size, head_dim = queries.shape
    scale = 1.0 / math.sqrt(head_dim)
    own_score = (
        jnp.einsum("skgd,skd->skg", queries, keys_new, preferred_element_type=jnp.float32) * scale
    )

    def block_scores(number):
        offset = number * block_len
        stored = lax.dynamic_slice_in_dim(cache_rows, offset, block_len, 1)
        keys = stored[:, :, 0].reshape(slot_count, block_len, groups_local, head_dim)
        values = stored[:, :, 1].reshape(slot_count, block_len, groups_local, head_dim)
        scores = (
            jnp.einsum("skgd,sjkd->skgj", queries, keys, preferred_element_type=jnp.float32) * scale
        )
        live_mask = (offset + jnp.arange(block_len, dtype=jnp.int32))[None, :] < slot_lengths[
            :, None
        ]
        scores = jnp.where(live_mask[:, None, None, :], scores, -jnp.inf)
        return (scores, values)

    def first_pass(number, running):
        maxima, totals = running
        scores, unused = block_scores(number)
        new_max = jnp.maximum(maxima, jnp.max(scores, axis=-1))
        totals = totals * jnp.exp(maxima - new_max) + jnp.sum(
            jnp.exp(scores - new_max[..., None]), axis=-1
        )
        return (new_max, totals)

    maxima, totals = lax.fori_loop(
        0, block_count, first_pass, (own_score, jnp.ones_like(own_score))
    )
    own_prob = (jnp.exp(own_score - maxima) / totals).astype(jnp.bfloat16)
    start_sum = (
        own_prob.astype(jnp.float32)[..., None] * values_new.astype(jnp.float32)[:, :, None, :]
    )

    def second_pass(number, summed):
        scores, values = block_scores(number)
        probs = (jnp.exp(scores - maxima[..., None]) / totals[..., None]).astype(jnp.bfloat16)
        return summed + jnp.einsum(
            "skgj,sjkd->skgd", probs, values, preferred_element_type=jnp.float32
        )

    return lax.fori_loop(0, block_count, second_pass, start_sum)


def per_device(residual, norm_gain, w_query, w_keyval, w_out, cache_rows, lengths, assignment):
    slot_count = cache_rows.shape[0]
    most_len = cache_rows.shape[1]
    channels = cache_rows.shape[3]
    query_cols = w_query.shape[1]
    width_local = w_query.shape[0]
    groups_local = channels // HD
    group_size = query_cols // channels
    row_count = slot_count * lax.axis_size(WIDE)
    inputs = residual.astype(jnp.float32)
    gain_local = norm_gain.astype(jnp.float32)
    gathered = collect(residual, "narrow", 0).astype(jnp.float32)
    squares = by_axis(jnp.sum(gathered * gathered, axis=1), WIDE)
    inverse_rms = lax.rsqrt(squares / D + 1e-05)
    normed = (gathered * inverse_rms[:, None] * gain_local[None, :]).astype(jnp.bfloat16)
    slot_rows = normed[assignment]
    keyval_flat = w_keyval.reshape(width_local, 2 * channels)
    combined = sum_by_axis(
        jnp.concatenate(
            [
                jnp.dot(slot_rows, w_query, preferred_element_type=jnp.float32),
                jnp.dot(slot_rows, keyval_flat, preferred_element_type=jnp.float32),
            ],
            axis=1,
        ),
        ("wide_0", "wide_1"),
        0,
    )
    query_raw = combined[:, :query_cols]
    keyval_raw = combined[:, query_cols:]
    owned_rows = lax.dynamic_slice_in_dim(assignment, lax.axis_index(WIDE) * slot_count, slot_count)
    slot_lengths = lengths[owned_rows]
    positions = slot_lengths.astype(jnp.float32)[:, None]
    queries = rotate(query_raw.reshape(slot_count, query_cols // HD, HD), positions).astype(
        jnp.bfloat16
    )
    queries = queries.reshape(slot_count, groups_local, group_size, HD)
    keyval_heads = keyval_raw.reshape(slot_count, 2, groups_local, HD)
    keys_new = rotate(keyval_heads[:, 0], positions).astype(jnp.bfloat16)
    values_new = keyval_heads[:, 1].astype(jnp.bfloat16)
    block_len = min(128, most_len)
    block_count = (jnp.max(slot_lengths) + block_len - 1) // block_len
    attended = attend(
        queries, keys_new, values_new, cache_rows, slot_lengths, block_count, block_len
    )
    attended = attended.reshape(slot_count, query_cols).astype(jnp.bfloat16)
    slot_update = jnp.dot(
        whole_of(attended, WIDE, (0, 1), 0), w_out, preferred_element_type=jnp.float32
    )
    slot_of = (
        jnp.zeros((row_count,), jnp.int32)
        .at[assignment]
        .set(jnp.arange(row_count, dtype=jnp.int32))
    )
    row_update = slot_update[slot_of]
    update = sum_at_owner(row_update, "narrow", 0)
    return (inputs + update).astype(jnp.bfloat16)


def solution(mesh):
    torus = Mesh(mesh.devices.reshape(4, 16, mesh.shape["narrow"]), ("wide_0", "wide_1", "narrow"))
    return jax.shard_map(
        per_device,
        mesh=torus,
        in_specs=(
            P("narrow", WIDE),
            P(WIDE),
            P(WIDE, "narrow"),
            P(WIDE, None, "narrow"),
            P("narrow", WIDE),
            P(WIDE, None, None, "narrow"),
            P(),
            P(),
        ),
        out_specs=P("narrow", WIDE),
        check_vma=False,
    )
```

profile of v0, /device:TPU:1, one launch (start us, length us, event | category | flops | bytes accessed | tf_op | source)
XLA Modules:
  0.0 228.0 jit_solution(15518554737774511760)
XLA Ops:
  6.5 1.5 broadcast_in_dim.52
  8.0 10.1 %all-to-all-start = ((bf16[8,32,256]{2,1,0:T(8,128)(2,1)}), bf16[8,32,256]{2,1,0:T(8,128)(2,1)S(1)}, u32[]{:S(2)}, u32[]{:S(2)}) async-start(bf16[8,32,256]{2,1,0:T(8,128)(2,1)} %broadcast_in_dim.52), calls=%async_computation | async-start | bytes 262144 | tf_op jit(solution)/shard_map/all_to_all | solution.py:16
  18.1 0.7 compare_select_fusion.1
  18.8 0.7 convert_element_type.74
  19.5 3.9 %all-to-all-done = bf16[8,32,256]{2,1,0:T(8,128)(2,1)S(1)} async-done(((bf16[8,32,256]{2,1,0:T(8,128)(2,1)}), bf16[8,32,256]{2,1,0:T(8,128)(2,1)S(1)}, u32[]{:S(2)}, u32[]{:S(2)}) %all-to-all-start) | async-done | bytes 131104 | tf_op jit(solution)/shard_map/all_to_all | solution.py:16
  23.4 0.1 multiply_reduce_fusion
  23.5 0.1 reduce_sum.50
  23.6 6.0 %psum.14 = f32[256]{0:T(256)S(1)} all-reduce(f32[256]{0:T(256)S(1)} %reduce_sum.50), channel_id=1, replica_groups=mesh['wide_0'=4,'wide_1'=16,'narrow'=8] {'wide_0'}, use_global_device_ids=true, to_apply=%region_1.0 | all-reduce | flops 256 | bytes 2048 | tf_op jit(solution)/shard_map/psum | solution.py:32
  29.5 27.5 %psum.15 = f32[256]{0:T(256)S(1)} all-reduce(f32[256]{0:T(256)S(1)} %psum.14), channel_id=1, replica_groups=mesh['wide_0'=4,'wide_1'=16,'narrow'=8] {'wide_1'}, use_global_device_ids=true, to_apply=%region_2.0 | all-reduce | flops 256 | bytes 2048 | tf_op jit(solution)/shard_map/psum | solution.py:32
  57.1 0.1 fusion.22
  57.2 1.2 gather_fusion
  58.4 0.2 fusion.23
  58.6 0.4 fusion.48
  59.0 0.2 pad_maximum_fusion
  59.2 21.6 %all_to_all.20 = f32[4,64,2304]{2,1,0:T(8,128)S(1)} all-to-all(f32[4,64,2304]{2,1,0:T(8,128)S(1)} %bitcast.104), channel_id=1, replica_groups=mesh['wide_0'=4,'wide_1'=16,'narrow'=8] {'wide_0'}, dimensions={0} | all-to-all | bytes 4718592 | tf_op jit(solution)/shard_map/all_to_all | solution.py:44
  80.8 1.0 reduce_sum.51
  81.8 2.0 reshape.321
  83.8 6.5 %all-to-all-start.2 = ((f32[16,4,2304]{2,1,0:T(4,128)}), f32[16,4,2304]{2,1,0:T(4,128)S(1)}, u32[]{:S(2)}, u32[]{:S(2)}) async-start(f32[16,4,2304]{2,1,0:T(4,128)} %reshape.321), calls=%async_computation.2 | async-start | bytes 1179648 | tf_op jit(solution)/shard_map/all_to_all | solution.py:44
  90.3 0.1 compare_select_fusion.2
  90.4 0.6 gather_fusion.1
  91.1 0.6 fusion.47
  92.3 1.6 copy.37
  93.9 0.1 multiply_cosine_fusion.1
  94.0 14.2 %all-to-all-done.2 = f32[16,4,2304]{2,1,0:T(4,128)S(1)} async-done(((f32[16,4,2304]{2,1,0:T(4,128)}), f32[16,4,2304]{2,1,0:T(4,128)S(1)}, u32[]{:S(2)}, u32[]{:S(2)}) %all-to-all-start.2) | async-done | bytes 589856 | tf_op jit(solution)/shard_map/all_to_all | solution.py:44
  108.2 0.1 reduce_sum.52
  108.4 0.1 fusion.42
  108.5 0.1 maximum_bitcast_fusion
  108.6 0.1 subtract_convert_fusion
  108.7 0.2 fusion.26
  108.9 0.1 pad_maximum_fusion.1
  109.0 1.1 while.22
  109.1 0.3 fusion.58
  109.3 0.2 exponential_reduce_fusion.2
  109.6 0.3 fusion.58
  109.9 0.2 exponential_reduce_fusion.2
  110.2 0.8 while.23
  110.3 0.3 fusion.60
  110.6 0.1 broadcast_compare_fusion.5
  110.7 0.3 fusion.60
  111.0 10.8 %all_gather.6 = bf16[4,4,2048]{2,1,0:T(4,128)(2,1)} all-gather(bf16[1,4,2048]{2,1,0:T(4,128)(2,1)S(1)} %convert_element_type.79), channel_id=1, replica_groups=mesh['wide_0'=4,'wide_1'=16,'narrow'=8] {'wide_0'}, dimensions={0}, use_global_device_ids=true | all-gather | bytes 81920 | tf_op jit(solution)/shard_map/all_gather | solution.py:57
  121.9 1.4 scatter_custom_fusion
  123.3 70.9 %all-gather.2.cloned.1.call-done = bf16[64,4,2048]{2,1,0:T(4,128)(2,1)} async-done(((bf16[4,4,2048]{2,1,0:T(4,128)(2,1)}), bf16[64,4,2048]{2,1,0:T(4,128)(2,1)}) %all-gather.2.cloned.1.call-update) | async-done | bytes 1048592 | tf_op jit(solution)/shard_map/all_gather | solution.py:57
  194.2 1.8 copy.39
  196.0 0.3 reshape_reshape.3
  196.3 1.7 fusion.49
  198.0 1.0 gather_fusion.2
  198.9 21.6 %all_to_all.21 = f32[8,32,256]{2,1,0:T(8,128)S(1)} all-to-all(f32[8,32,256]{2,1,0:T(8,128)S(1)} %bitcast.105), channel_id=1, replica_groups=mesh['wide_0'=4,'wide_1'=16,'narrow'=8] {'narrow'}, dimensions={0} | all-to-all | bytes 524288 | tf_op jit(solution)/shard_map/all_to_all | solution.py:44
  220.5 0.6 add_convert_fusion
  (45 shorter events, 0.6 us)
Async XLA Ops:
  6.5 52.0 %copy-start = (bf16[256,2048]{1,0:T(8,128)(2,1)S(1)}, bf16[256,2048]{1,0:T(8,128)(2,1)}, u32[]{:S(2)}) copy-start(bf16[256,2048]{1,0:T(8,128)(2,1)} %param.14) | copy-start | bytes 3145732
  6.5 51.8 %copy-start.2 = (bf16[256,2,128]{2,1,0:T(2,128)(2,1)S(1)}, bf16[256,2,128]{2,1,0:T(2,128)(2,1)}, u32[]{:S(2)}) copy-start(bf16[256,2,128]{2,1,0:T(2,128)(2,1)} %param.15) | copy-start | bytes 393220
  8.0 15.4 %all-to-all-start = ((bf16[8,32,256]{2,1,0:T(8,128)(2,1)}), bf16[8,32,256]{2,1,0:T(8,128)(2,1)S(1)}, u32[]{:S(2)}, u32[]{:S(2)}) async-start(bf16[8,32,256]{2,1,0:T(8,128)(2,1)} %broadcast_in_dim.52), calls=%async_computation | async-start | bytes 262144 | tf_op jit(solution)/shard_map/all_to_all | solution.py:16
  80.8 9.5 %copy-start.4 = (s32[256]{0:T(256)S(1)}, s32[256]{0:T(256)}, u32[]{:S(2)}) copy-start(s32[256]{0:T(256)} %param.19) | copy-start | bytes 3076
  80.8 9.6 %copy-start.1 = (s32[256]{0:T(256)S(1)}, s32[256]{0:T(256)}, u32[]{:S(2)}) copy-start(s32[256]{0:T(256)} %param.18) | copy-start | bytes 3076
  83.8 24.4 %all-to-all-start.2 = ((f32[16,4,2304]{2,1,0:T(4,128)}), f32[16,4,2304]{2,1,0:T(4,128)S(1)}, u32[]{:S(2)}, u32[]{:S(2)}) async-start(f32[16,4,2304]{2,1,0:T(4,128)} %reshape.321), calls=%async_computation.2 | async-start | bytes 1179648 | tf_op jit(solution)/shard_map/all_to_all | solution.py:44
  90.3 103.9 %all-gather.2.cloned.1.call-start = ((), (), s32[]{:S(2)}) async-start(), calls=%async_computation.4 | async-start | bytes 1114112 | tf_op jit(solution)/shard_map/all_gather | solution.py:57
  198.0 22.6 %copy-start.3 = (bf16[32,256]{1,0:T(8,128)(2,1)S(1)}, bf16[32,256]{1,0:T(8,128)(2,1)}, u32[]{:S(2)}) copy-start(bf16[32,256]{1,0:T(8,128)(2,1)} %param.12) | copy-start | bytes 49156
Sparse Core Ops, SparseCore 0:
  122.0 72.1 all-gather.1
where the time goes:
time: 229 us; the launch traced here: 228 us
  waiting for transfers between devices  89.1 us (39%)
  blocking collectives  87.5 us (38%)
  starting transfers between devices  16.6 us (7%)
  between operations  14.2 us (6%)
  local copies, waits for them, and re-layouts  11.5 us (5%)
  other arithmetic  5.49 us (2%)
  matrix products  3.6 us (2%)
    all_gather x1, waiting for transfers between devices, gather_in_order(): tiles = lax.all_gather(tiles, axes[k], axis=0, tiled=True)  70.9 us
    all_to_all x2, blocking collectives, sum_at_owner(): lax.all_to_all(tiles, axis, split_axis=0, concat_axis=0, tiled=True)  43.2 us
    psum x2, blocking collectives, by_axis(): shard = lax.psum(shard, axis)  33.5 us
    all_to_all x1, waiting for transfers between devices, sum_at_owner(): lax.all_to_all(tiles, axis, split_axis=0, concat_axis=0, tiled=True)  14.2 us
    all_gather x1, blocking collectives, gather_in_order(): tiles = lax.all_gather(tiles, axes[k], axis=0, tiled=True)  10.8 us
    all_to_all x1, starting transfers between devices, copy_for_each(): return lax.all_to_all(copies, axis, split_axis=0, concat_axis=0, tiled=True)  10.1 us
    all_to_all x1, starting transfers between devices, sum_at_owner(): lax.all_to_all(tiles, axis, split_axis=0, concat_axis=0, tiled=True)  6.45 us
  transfers between devices with their start and end apart: 3, of which 3 were waited for; matrix products, arithmetic and copies ran while one was open for 3% of the time, Pallas kernels for 0%

commit v1 on v0

v1 whole, which is shorter than its diff:
```python
import functools
import math

import jax
import jax.numpy as jnp
import numpy as np
from jax import lax
from jax.experimental import pallas as pl
from jax.experimental.pallas import tpu as pltpu
from jax.sharding import Mesh
from jax.sharding import PartitionSpec as P

HD = 128
MESH = pl.DeviceIdType.MESH
F32 = jnp.float32
BF16 = jnp.bfloat16


def rotation_table(most):
    half = HD // 2
    exponents = -(np.arange(half, dtype=np.float32) * np.float32(2.0) / np.float32(HD))
    freqs = np.power(np.float32(500000.0), exponents).astype(np.float32)
    rows = (most + 8) // 8 * 8
    angles = (np.arange(rows, dtype=np.float32)[:, None] * freqs[None, :]).astype(np.float32)
    angles = angles.astype(np.float64)
    return np.concatenate([np.cos(angles), np.sin(angles)], axis=1).astype(np.float32)


def dot(a, b):
    return lax.dot_general(a, b, (((1,), (0,)), ((), ())), preferred_element_type=F32)


def dot_t(a, b):
    return lax.dot_general(a, b, (((1,), (1,)), ((), ())), preferred_element_type=F32)


def by_distance(count):
    return sorted(range(1, count), key=lambda d: min(d, count - d))


def kernel(
    nx, nz, nn, width,
    lens, asg, res_h, gain_ref, asg_ref, wq_h, wkv_h, wo_h, cache_h, tab_h,
    out_ref,
    nres, gains, wq, wkv, kvs, kvw, wo, cache, kc, vc, tab,
    zin, nsq, pz, pr, sres, nrm, part, rbuf, lbuf, xs, xin, q_ref, ab, ag, att, nst, nin,
    loc, xr_s, xr_r, xg_s, xg_r, xw_s, xw_r, kv_s, kv_r, ng_s, ng_r,
    zs_s, zs_r, ns_s, ns_r, rr_s, rr_r, lr_s, lr_r, xe_s, xe_r,
    az_s, az_r, ax_s, ax_r, no_s, no_r,
):
    x, z, n = lax.axis_index("x"), lax.axis_index("z"), lax.axis_index("narrow")
    rows = pz.shape[0]
    rows_n = rows // nn
    slots = xs.shape[1]
    per_z = nx * slots
    qcols = wq.shape[2]
    kw = wq.shape[1]
    most = kc.shape[1]
    heads = q_ref.shape[1]
    heads_x = heads // nx
    w_own = x * nz + z

    def remote(src, dst, ss, rs, dev):
        return pltpu.make_async_remote_copy(
            src_ref=src, dst_ref=dst, send_sem=ss, recv_sem=rs, device_id=dev, device_id_type=MESH
        )

    def at_x(d):
        return lax.rem(x + d, nx)

    def at_z(d):
        return lax.rem(z + d, nz)

    def at_n(d):
        return lax.rem(n + d, nn)

    def wq_part(t):
        return wq_h.at[:, pl.ds(pl.multiple_of(t * qcols, qcols), qcols)]

    local = [
        pltpu.make_async_copy(wkv_h, wkv, loc.at[0]),
        pltpu.make_async_copy(res_h, nres.at[n, x], loc.at[1]),
        pltpu.make_async_copy(wq_part(x), wq.at[x], loc.at[2]),
        pltpu.make_async_copy(cache_h, cache, loc.at[3]),
        pltpu.make_async_copy(wo_h, wo, loc.at[4]),
        pltpu.make_async_copy(tab_h, tab, loc.at[5]),
    ]
    barrier = pltpu.get_barrier_semaphore()
    for d in reversed(by_distance(nz)):
        pl.semaphore_signal(barrier, inc=1, device_id={"z": at_z(d)}, device_id_type=MESH)
    for d in range(1, nx):
        pl.semaphore_signal(barrier, inc=1, device_id={"x": at_x(d)}, device_id_type=MESH)
    for d in range(1, nn):
        pl.semaphore_signal(barrier, inc=1, device_id={"narrow": at_n(d)}, device_id_type=MESH)
    for copy in local:
        copy.start()

    a_row = asg_ref[...]
    i_sub = lax.broadcasted_iota(jnp.int32, (rows, rows), 0)
    i_lane = lax.broadcasted_iota(jnp.int32, (rows, rows), 1)
    zz, rest = i_sub // per_z, i_sub % per_z
    slot_of = ((rest // slots) * nz + zz) * slots + rest % slots
    a_col = jnp.sum(
        jnp.where(i_lane == slot_of, a_row.astype(F32), 0.0), axis=1, keepdims=True
    ).astype(jnp.int32)
    pick = i_lane == a_col
    pz[...] = jnp.where(pick, 1.0, 0.0).astype(BF16)
    pr[...] = jnp.where(i_sub == a_row, 1.0, 0.0).astype(BF16)
    gains[x] = gain_ref[...].astype(F32)

    e_row = lax.broadcasted_iota(jnp.int32, (kw, 2 * kw), 0)
    e_col = lax.broadcasted_iota(jnp.int32, (kw, 2 * kw), 1)
    e0 = jnp.where(e_col == 2 * e_row, 1.0, 0.0).astype(BF16)
    e1 = jnp.where(e_col == 2 * e_row + 1, 1.0, 0.0).astype(BF16)
    local[0].wait()
    kvs[0] = dot(e0, wkv[...]).astype(BF16)
    kvs[1] = dot(e1, wkv[...]).astype(BF16)

    pl.semaphore_wait(barrier, (nx - 1) + (nz - 1) + (nn - 1))

    sends = []

    def send(copy):
        copy.start()
        sends.append(copy)

    for d in range(1, nx):
        dev = {"x": at_x(d)}
        send(remote(res_h, nres.at[n, x], xr_s.at[d], xr_r.at[d], dev))
        send(remote(gains.at[x], gains.at[x], xg_s.at[d], xg_r.at[d], dev))
    for d in range(1, nx):
        send(remote(wq_part(at_x(d)), wq.at[x], xw_s.at[d], xw_r.at[d], {"x": at_x(d)}))
    kv_slot = lax.rem(x, 2)
    k_copy = remote(kvs.at[0], kvw.at[kv_slot], kv_s.at[0], kv_r.at[kv_slot], {"x": x // 2})
    v_copy = remote(kvs.at[1], kvw.at[kv_slot], kv_s.at[1], kv_r.at[kv_slot], {"x": 2 + x // 2})

    @pl.when(x != 0)
    def _():
        k_copy.start()

    @pl.when(x == 0)
    def _():
        kvw[0] = kvs[0]

    @pl.when(x != nx - 1)
    def _():
        v_copy.start()

    @pl.when(x == nx - 1)
    def _():
        kvw[1] = kvs[1]

    local[1].wait()
    for d in range(1, nx):
        src = at_x(nx - d)
        remote(res_h, nres.at[n, src], xr_s.at[d], xr_r.at[d], {"x": src}).wait_recv()
    for d in range(1, nn):
        send(remote(nres.at[n], nres.at[n], ng_s.at[d], ng_r.at[d], {"narrow": at_n(d)}))

    squares = jnp.zeros((rows_n, 1), F32)
    for k in range(nx):
        block = nres[n, k].astype(F32)
        squares = squares + jnp.sum(block * block, axis=1, keepdims=True)
    r_sub = lax.broadcasted_iota(jnp.int32, (rows_n, rows), 0)
    r_lane = lax.broadcasted_iota(jnp.int32, (rows_n, rows), 1)
    zin[z] = jnp.sum(jnp.where(r_lane == r_sub + n * rows_n, squares, 0.0), axis=0, keepdims=True)
    for d in reversed(by_distance(nz)):
        send(remote(zin.at[z], zin.at[z], zs_s.at[d], zs_r.at[d], {"z": at_z(d)}))

    local[3].wait()
    step = kw
    for j in range(slots):
        for b in range(most // step):
            block = cache[pl.ds((j * most + b * step) * 2, 2 * step), :]
            kc[j, b * step : (b + 1) * step, :] = dot(e0, block).astype(BF16)
            vc[j, b * step : (b + 1) * step, :] = dot(e1, block).astype(BF16)

    for d in range(1, nn):
        src = at_n(nn - d)
        remote(nres.at[src], nres.at[src], ng_s.at[d], ng_r.at[d], {"narrow": src}).wait_recv()
    for k in range(nx):
        block = nres[:, k].reshape(rows, kw)
        sres[:, k * kw : (k + 1) * kw] = dot(pz[...], block).astype(BF16)

    for d in range(1, nz):
        src = at_z(nz - d)
        remote(zin.at[src], zin.at[src], zs_s.at[d], zs_r.at[d], {"z": src}).wait_recv()
    nsq[n] = jnp.sum(zin[...], axis=0)
    for d in range(1, nn):
        send(remote(nsq.at[n], nsq.at[n], ns_s.at[d], ns_r.at[d], {"narrow": at_n(d)}))
    for d in range(1, nn):
        src = at_n(nn - d)
        remote(nsq.at[src], nsq.at[src], ns_s.at[d], ns_r.at[d], {"narrow": src}).wait_recv()
    sums = jnp.sum(nsq[...], axis=0)
    sum_col = jnp.sum(jnp.where(pz[...].astype(F32) > 0.5, sums, 0.0), axis=1, keepdims=True)
    inverse = lax.rsqrt(sum_col / width + 1e-05)

    for d in range(1, nx):
        src = at_x(nx - d)
        remote(gains.at[src], gains.at[src], xg_s.at[d], xg_r.at[d], {"x": src}).wait_recv()
    for k in range(nx):
        block = sres[:, k * kw : (k + 1) * kw].astype(F32)
        nrm[:, k * kw : (k + 1) * kw] = (block * inverse * gains[k]).astype(BF16)

    local[2].wait()
    for d in range(1, nx):
        src = at_x(nx - d)
        remote(wq_part(src), wq.at[src], xw_s.at[d], xw_r.at[d], {"x": src}).wait_recv()

    @pl.when(x != 0)
    def _():
        remote(kvs.at[0], kvw.at[0], kv_s.at[0], kv_r.at[0], {"x": x // 2}).wait_recv()

    @pl.when(x != nx - 1)
    def _():
        remote(kvs.at[0], kvw.at[1], kv_s.at[0], kv_r.at[1], {"x": x // 2}).wait_recv()

    total = dot(nrm[:, :kw], wq[0])
    for k in range(1, nx):
        total = total + dot(nrm[:, k * kw : (k + 1) * kw], wq[k])
    part[:, :, :qcols] = total.reshape(nz, per_z, qcols)
    half = nrm[:, pl.ds(pl.multiple_of(lax.rem(x, 2) * 2 * kw, 2 * kw), 2 * kw)]
    kv_part = dot(half[:, :kw], kvw[0]) + dot(half[:, kw:], kvw[1])
    part[:, :, qcols:] = kv_part.reshape(nz, per_z, HD)

    right, left = {"z": at_z(1)}, {"z": at_z(nz - 1)}
    r_steps, l_steps = nz // 2, nz - 1 - nz // 2
    cols = part.shape[2]
    cuts = [(0, 384), (384, cols)]

    def r_copy(s, c):
        lo, hi = cuts[c]
        owner = at_z(r_steps - s)
        src = part.at[owner, :, lo:hi] if s == 0 else rbuf.at[s - 1, :, lo:hi]
        return remote(src, rbuf.at[s, :, lo:hi], rr_s.at[s, c], rr_r.at[s, c], right)

    def l_copy(s, c):
        lo, hi = cuts[c]
        owner = at_z(nz - l_steps + s)
        src = part.at[owner, :, lo:hi] if s == 0 else lbuf.at[s - 1, :, lo:hi]
        return remote(src, lbuf.at[s, :, lo:hi], lr_s.at[s, c], lr_r.at[s, c], left)

    for c in range(len(cuts)):
        send(r_copy(0, c))
        if l_steps > 0:
            send(l_copy(0, c))
    for s in range(r_steps):
        for c, (lo, hi) in enumerate(cuts):
            r_copy(s, c).wait_recv()
            if s + 1 < r_steps:
                owner = at_z(r_steps - s - 1)
                rbuf[s, :, lo:hi] = rbuf[s, :, lo:hi] + part[owner, :, lo:hi]
                send(r_copy(s + 1, c))
            if s < l_steps:
                l_copy(s, c).wait_recv()
                if s + 1 < l_steps:
                    owner = at_z(nz - l_steps + s + 1)
                    lbuf[s, :, lo:hi] = lbuf[s, :, lo:hi] + part[owner, :, lo:hi]
                    send(l_copy(s + 1, c))
    own = part[z] + rbuf[r_steps - 1]
    if l_steps > 0:
        own = own + lbuf[l_steps - 1]
    for k in range(nx):
        xs[k] = own[k * slots : (k + 1) * slots]
    for d in range(1, nx):
        send(remote(xs.at[at_x(d)], xin.at[x], xe_s.at[d], xe_r.at[d], {"x": at_x(d)}))
    xin[x] = xs[x]

    local[5].wait()
    lengths = [lens[asg[w_own * slots + j]] for j in range(slots)]
    angles = jnp.concatenate([tab[pl.ds(lengths[j], 1), :] for j in range(slots)], axis=0)
    turned = pltpu.roll(angles, HD // 2, 1)
    lane = lax.broadcasted_iota(jnp.int32, (slots, HD), 1)
    cosine = jnp.where(lane < HD // 2, angles, turned)
    sine = jnp.where(lane < HD // 2, -turned, angles)

    def rotate(v):
        return (v * cosine + pltpu.roll(v, HD // 2, 1) * sine).astype(BF16).astype(F32)

    for d in range(1, nx):
        src = at_x(nx - d)
        remote(xs.at[0], xin.at[src], xe_s.at[d], xe_r.at[d], {"x": src}).wait_recv()
    for k in range(nx):
        for i in range(heads_x):
            turned_query = rotate(xin[k, :, i * HD : (i + 1) * HD])
            for j in range(slots):
                q_ref[j, k * heads_x + i : k * heads_x + i + 1, :] = turned_query[j : j + 1]
    keys_new = rotate(xin[0, :, qcols:] + xin[1, :, qcols:])
    values_new = (xin[2, :, qcols:] + xin[3, :, qcols:]).astype(BF16).astype(F32)

    scale = 1.0 / math.sqrt(HD)
    position = lax.broadcasted_iota(jnp.int32, (heads, most), 1)
    for j in range(slots):
        query = q_ref[j]
        own_score = jnp.sum(query * keys_new[j : j + 1], axis=1, keepdims=True) * scale
        scores = dot_t(query.astype(BF16), kc[j]) * scale
        scores = jnp.where(position < lengths[j], scores, -jnp.inf)
        top = jnp.maximum(jnp.max(scores, axis=1, keepdims=True), own_score)
        weights = jnp.exp(scores - top)
        own_weight = jnp.exp(own_score - top)
        totals = jnp.sum(weights, axis=1, keepdims=True) + own_weight
        probs = (weights / totals).astype(BF16)
        own_prob = (own_weight / totals).astype(BF16).astype(F32)
        attended = dot(probs, vc[j]) + own_prob * values_new[j : j + 1]
        for h in range(heads):
            ab[j : j + 1, h * HD : (h + 1) * HD] = attended[h : h + 1]
    ag[w_own] = ab[...].astype(BF16)

    for d in reversed(by_distance(nz)):
        send(remote(ag.at[w_own], ag.at[w_own], az_s.at[d], az_r.at[d], {"z": at_z(d)}))
    for d in [0] + by_distance(nz):
        src_z = at_z(nz - d)
        block = x * nz + src_z
        if d > 0:
            remote(ag.at[block], ag.at[block], az_s.at[d], az_r.at[d], {"z": src_z}).wait_recv()
        for e in range(1, nx):
            send(remote(ag.at[block], ag.at[block], ax_s.at[d, e], ax_r.at[d, e], {"x": at_x(e)}))
    local[4].wait()
    for d in [0] + by_distance(nz):
        for e in range(1, nx):
            src_x = at_x(nx - e)
            block = src_x * nz + at_z(nz - d)
            remote(ag.at[block], ag.at[block], ax_s.at[d, e], ax_r.at[d, e], {"x": src_x}).wait_recv()

    group = 16 // slots
    for g in range(rows // 16):
        pieces = [ag[g * group + i].astype(F32) for i in range(group)]
        att[g * 16 : (g + 1) * 16, :] = jnp.concatenate(pieces, axis=0).astype(BF16)
    tile = 512
    update = jnp.zeros((rows, wo.shape[1]), F32)
    for k in range(att.shape[1] // tile):
        picked = dot(pr[...], att[:, k * tile : (k + 1) * tile]).astype(BF16)
        update = update + dot(picked, wo[k * tile : (k + 1) * tile, :])
    nst[...] = update.reshape(nn, rows_n, wo.shape[1])
    for d in range(1, nn):
        send(remote(nst.at[at_n(d)], nin.at[n], no_s.at[d], no_r.at[d], {"narrow": at_n(d)}))
    nin[n] = nst[n]
    for d in range(1, nn):
        src = at_n(nn - d)
        remote(nst.at[0], nin.at[src], no_s.at[d], no_r.at[d], {"narrow": src}).wait_recv()
    result = nin[0]
    for k in range(1, nn):
        result = result + nin[k]
    out_ref[...] = (nres[n, x].astype(F32) + result).astype(BF16)

    for copy in sends:
        copy.wait_send()

    @pl.when(x != 0)
    def _():
        k_copy.wait_send()

    @pl.when(x != nx - 1)
    def _():
        v_copy.wait_send()


def per_device(nx, nz, nn, table, residual, norm_gain, w_query, w_keyval, w_out, cache_rows, lengths, assignment):
    slots, most, _, channels = cache_rows.shape
    kw, query_cols = w_query.shape
    rows_n = residual.shape[0]
    rows = rows_n * nn
    qcols = query_cols // nx
    cols = qcols + HD
    heads = query_cols // HD
    r_steps, l_steps = nz // 2, max(nz - 1 - nz // 2, 1)
    width = kw * nx * nz
    anywhere = pl.BlockSpec(memory_space=pl.ANY)
    vmem = pl.BlockSpec(memory_space=pltpu.VMEM)
    smem = pl.BlockSpec(memory_space=pltpu.SMEM)
    dma = pltpu.SemaphoreType.DMA
    scratch = [
        pltpu.VMEM((nn, nx, rows_n, kw), BF16),
        pltpu.VMEM((nx, 1, kw), F32),
        pltpu.VMEM((nx, kw, qcols), BF16),
        pltpu.VMEM((2 * kw, HD), BF16),
        pltpu.VMEM((2, kw, HD), BF16),
        pltpu.VMEM((2, kw, HD), BF16),
        pltpu.VMEM(w_out.shape, BF16),
        pltpu.VMEM((slots * most * 2, HD), BF16),
        pltpu.VMEM((slots, most, HD), BF16),
        pltpu.VMEM((slots, most, HD), BF16),
        pltpu.VMEM(table.shape, F32),
        pltpu.VMEM((nz, 1, rows), F32),
        pltpu.VMEM((nn, 1, rows), F32),
        pltpu.VMEM((rows, rows), BF16),
        pltpu.VMEM((rows, rows), BF16),
        pltpu.VMEM((rows, nx * kw), BF16),
        pltpu.VMEM((rows, nx * kw), BF16),
        pltpu.VMEM((nz, nx * slots, cols), F32),
        pltpu.VMEM((r_steps, nx * slots, cols), F32),
        pltpu.VMEM((l_steps, nx * slots, cols), F32),
        pltpu.VMEM((nx, slots, cols), F32),
        pltpu.VMEM((nx, slots, cols), F32),
        pltpu.VMEM((slots, heads, HD), F32),
        pltpu.VMEM((slots, query_cols), F32),
        pltpu.VMEM((nx * nz, slots, query_cols), BF16),
        pltpu.VMEM((rows, query_cols), BF16),
        pltpu.VMEM((nn, rows_n, w_out.shape[1]), F32),
        pltpu.VMEM((nn, rows_n, w_out.shape[1]), F32),
        dma((6,)),
        dma((nx,)), dma((nx,)), dma((nx,)), dma((nx,)), dma((nx,)), dma((nx,)),
        dma((2,)), dma((2,)),
        dma((nn,)), dma((nn,)),
        dma((nz,)), dma((nz,)),
        dma((nn,)), dma((nn,)),
        dma((r_steps, 2)), dma((r_steps, 2)), dma((l_steps, 2)), dma((l_steps, 2)),
        dma((nx,)), dma((nx,)),
        dma((nz,)), dma((nz,)), dma((nz, nx)), dma((nz, nx)),
        dma((nn,)), dma((nn,)),
    ]
    return pl.pallas_call(
        functools.partial(kernel, nx, nz, nn, width),
        out_shape=jax.ShapeDtypeStruct(residual.shape, BF16),
        in_specs=[smem, smem, anywhere, vmem, vmem] + [anywhere] * 5,
        out_specs=vmem,
        scratch_shapes=scratch,
        compiler_params=pltpu.CompilerParams(
            collective_id=0, has_side_effects=True, vmem_limit_bytes=60 * 1024 * 1024
        ),
        name="decode_block",
    )(
        lengths,
        assignment,
        residual,
        norm_gain.reshape(1, -1),
        assignment.reshape(1, -1),
        w_query,
        w_keyval.reshape(2 * kw, channels),
        w_out,
        cache_rows.reshape(slots * most * 2, channels),
        table,
    )


def solution(mesh):
    nx, nn = 4, mesh.shape["narrow"]
    nz = mesh.shape["wide"] // nx
    torus = Mesh(mesh.devices.reshape(nx, nz, nn), ("x", "z", "narrow"))
    wide = ("x", "z")

    def run(residual, norm_gain, w_query, w_keyval, w_out, cache_rows, lengths, assignment):
        table = jnp.asarray(rotation_table(cache_rows.shape[1]))
        body = jax.shard_map(
            lambda table, *args: per_device(nx, nz, nn, table, *args),
            mesh=torus,
            in_specs=(
                P(),
                P("narrow", wide),
                P(wide),
                P(wide, "narrow"),
                P(wide, None, "narrow"),
                P("narrow", wide),
                P(wide, None, None, "narrow"),
                P(),
                P(),
            ),
            out_specs=P("narrow", wide),
            check_vma=False,
        )
        return body(table, residual, norm_gain, w_query, w_keyval, w_out, cache_rows, lengths, assignment)

    return run
```

time: 229 us -> 95.5 us (0.42)
  Pallas kernels: 0 us -> 92.7 us
  waiting for transfers between devices: 89.1 us -> 0 us
  blocking collectives: 87.5 us -> 0 us
  starting transfers between devices: 16.6 us -> 0 us
  between operations: 14.2 us -> 0.01 us
  local copies, waits for them, and re-layouts: 11.5 us -> 2.54 us
  other arithmetic: 5.49 us -> 0 us
  matrix products: 3.6 us -> 0 us
    pallas_call x0 -> x1, Pallas kernels: none -> 92.7 us  [per_device(): pl.pallas_call(functools.partial(kernel, nx, nz, nn, width), out_shape=ja...]
    all_gather x1 -> x0, waiting for transfers between devices: 70.9 us -> none  [gather_in_order(): tiles = lax.all_gather(tiles, axes[k], axis=0, tiled=True)]
    all_to_all x2 -> x0, blocking collectives: 43.2 us -> none  [sum_at_owner(): lax.all_to_all(tiles, axis, split_axis=0, concat_axis=0, tiled=True)]
    psum x2 -> x0, blocking collectives: 33.5 us -> none  [by_axis(): shard = lax.psum(shard, axis)]
    all_to_all x2 -> x0, waiting for transfers between devices: 18.1 us -> none  [the longest x1 14.2 us: sum_at_owner(): lax.all_to_all(tiles, axis, split_axis=0, concat_axis=0, tiled=True)]
    all_to_all x2 -> x0, starting transfers between devices: 16.6 us -> none  [the longest x1 10.1 us: copy_for_each(): return lax.all_to_all(copies, axis, split_axis=0, concat_axis=0, tiled=True)]
    all_gather x1 -> x0, blocking collectives: 10.8 us -> none  [gather_in_order(): tiles = lax.all_gather(tiles, axes[k], axis=0, tiled=True)]
    dot_general x8 -> x0, matrix products: 3.6 us -> none  [the longest x1 1.66 us: per_device(): jnp.dot(whole_of(attended, WIDE, (0, 1), 0), w_out, preferred_element_typ...]
  transfers between devices with their start and end apart: 3 -> 0, of which waited for: 3 -> 0; matrix products, arithmetic and copies ran while one was open for 3% -> 0% of each run, Pallas kernels for 0% -> 0%
where the time goes in v1:
time: 95.5 us; the launch traced here: 95.2 us
  Pallas kernels  92.7 us (97%)
  local copies, waits for them, and re-layouts  2.54 us (3%)
    pallas_call x1, Pallas kernels, per_device(): pl.pallas_call(functools.partial(kernel, nx, nz, nn, width), out_shape=ja...  92.7 us

profile of v1, /device:TPU:1, one launch (start us, length us, event | category | flops | bytes accessed | tf_op | source)
XLA Modules:
  0.0 95.2 jit_solution(8047208551158973338)
XLA Ops:
  0.0 1.2 %reshape.12.gain_ref = bf16[1,256]{1,0:T(2,128)(2,1)} reshape(bf16[256]{0:T(256)(128)(2,1)} %param.10) | data formatting | bytes 1024 | tf_op jit(solution)/shard_map/reshape | solution.py:426
  1.2 92.7 %decode_block.1 = bf16[32,256]{1,0:T(8,128)(2,1)} custom-call(s32[256]{0:T(256)} %lens.1, s32[256]{0:T(256)} %asg.1, bf16[32,256]{1,0:T(8,128)(2,1)} %res_h.1, bf16[1,256]{1,0:T(2,128)(2,1)} %reshape.12.gain_ref, s32[1,256]{1,0:T(1,128)} %bitcast.5, bf16[256,2048]{1,0:T(8,128)(2,1)} %wq_h.1, bf16[512,128]{1,0:T(8,128)(2,1)} %bitcast.4, ...), custom_call_target="tpu_custom_call" | custom-call | tf_op jit(solution)/shard_map/decode_block/pallas_call | solution.py:412
  93.9 1.3 %copy.11 = bf16[32,256]{1,0:T(8,128)(2,1)} copy(bf16[32,256]{1,0:T(8,128)(2,1)} %decode_block.1) | data formatting | bytes 32768

commit v2 on v1

--- a/solution.py
+++ b/solution.py
@@ -40,19 +40,23 @@
 
 def kernel(
     nx, nz, nn, width,
-    lens, asg, res_h, gain_ref, asg_ref, wq_h, wkv_h, wo_h, cache_h, tab_h,
+    lens, asg, res_h, gain_h, asg_ref, wq_h, wkv_h, wo_h, cache_h, tab_h,
     out_ref,
     nres, gains, wq, wkv, kvs, kvw, wo, cache, kc, vc, tab,
-    zin, nsq, pz, pr, sres, nrm, part, rbuf, lbuf, xs, xin, q_ref, ab, ag, att, nst, nin,
+    gain_v, zin, nsq, pz, pr, sres, nrm, part, rbuf, lbuf, xs, xin, q_ref, ab, ag, att, nst, nin,
     loc, xr_s, xr_r, xg_s, xg_r, xw_s, xw_r, kv_s, kv_r, ng_s, ng_r,
     zs_s, zs_r, ns_s, ns_r, rr_s, rr_r, lr_s, lr_r, xe_s, xe_r,
     az_s, az_r, ax_s, ax_r, no_s, no_r,
 ):
     x, z, n = lax.axis_index("x"), lax.axis_index("z"), lax.axis_index("narrow")
+    y, c = n // 2, n % 2
+    ny = nn // 2
+    turn = 1 - 2 * c
     rows = pz.shape[0]
     rows_n = rows // nn
-    slots = xs.shape[1]
+    slots = xs.shape[2]
     per_z = nx * slots
+    pieces = part.shape[1]
     qcols = wq.shape[2]
     kw = wq.shape[1]
     most = kc.shape[1]
@@ -77,6 +81,7 @@
     def wq_part(t):
         return wq_h.at[:, pl.ds(pl.multiple_of(t * qcols, qcols), qcols)]
 
+    plane = [(dx, dn) for dx in range(nx) for dn in range(nn) if dx + dn > 0]
     local = [
         pltpu.make_async_copy(wkv_h, wkv, loc.at[0]),
         pltpu.make_async_copy(res_h, nres.at[n, x], loc.at[1]),
@@ -84,14 +89,14 @@
         pltpu.make_async_copy(cache_h, cache, loc.at[3]),
         pltpu.make_async_copy(wo_h, wo, loc.at[4]),
         pltpu.make_async_copy(tab_h, tab, loc.at[5]),
+        pltpu.make_async_copy(gain_h, gain_v, loc.at[6]),
     ]
     barrier = pltpu.get_barrier_semaphore()
     for d in reversed(by_distance(nz)):
         pl.semaphore_signal(barrier, inc=1, device_id={"z": at_z(d)}, device_id_type=MESH)
-    for d in range(1, nx):
-        pl.semaphore_signal(barrier, inc=1, device_id={"x": at_x(d)}, device_id_type=MESH)
-    for d in range(1, nn):
-        pl.semaphore_signal(barrier, inc=1, device_id={"narrow": at_n(d)}, device_id_type=MESH)
+    for dx, dn in plane:
+        dev = {"x": at_x(dx), "narrow": at_n(dn)}
+        pl.semaphore_signal(barrier, inc=1, device_id=dev, device_id_type=MESH)
     for copy in local:
         copy.start()
 
@@ -106,7 +111,15 @@
     pick = i_lane == a_col
     pz[...] = jnp.where(pick, 1.0, 0.0).astype(BF16)
     pr[...] = jnp.where(i_sub == a_row, 1.0, 0.0).astype(BF16)
-    gains[x] = gain_ref[...].astype(F32)
+    local[6].wait()
+    gains[x] = gain_v[...].astype(F32).reshape(1, kw)
+
+    local[1].wait()
+    block = nres[n, x].astype(F32)
+    squares = jnp.sum(block * block, axis=1, keepdims=True)
+    r_sub = lax.broadcasted_iota(jnp.int32, (rows_n, rows), 0)
+    r_lane = lax.broadcasted_iota(jnp.int32, (rows_n, rows), 1)
+    zin[z] = jnp.sum(jnp.where(r_lane == r_sub + n * rows_n, squares, 0.0), axis=0, keepdims=True)
 
     e_row = lax.broadcasted_iota(jnp.int32, (kw, 2 * kw), 0)
     e_col = lax.broadcasted_iota(jnp.int32, (kw, 2 * kw), 1)
@@ -116,7 +129,7 @@
     kvs[0] = dot(e0, wkv[...]).astype(BF16)
     kvs[1] = dot(e1, wkv[...]).astype(BF16)
 
-    pl.semaphore_wait(barrier, (nx - 1) + (nz - 1) + (nn - 1))
+    pl.semaphore_wait(barrier, len(plane) + nz - 1)
 
     sends = []
 
@@ -124,6 +137,8 @@
         copy.start()
         sends.append(copy)
 
+    for d in reversed(by_distance(nz)):
+        send(remote(zin.at[z], zin.at[z], zs_s.at[d], zs_r.at[d], {"z": at_z(d)}))
     for d in range(1, nx):
         dev = {"x": at_x(d)}
         send(remote(res_h, nres.at[n, x], xr_s.at[d], xr_r.at[d], dev))
@@ -150,22 +165,20 @@
     def _():
         kvw[1] = kvs[1]
 
-    local[1].wait()
+    def narrow(dy, core):
+        return lax.rem(y + dy + ny, ny) * 2 + core
+
+    def row_copy(k, src, to):
+        return remote(nres.at[src], nres.at[src], ng_s.at[k], ng_r.at[k], {"narrow": to})
+
     for d in range(1, nx):
         src = at_x(nx - d)
         remote(res_h, nres.at[n, src], xr_s.at[d], xr_r.at[d], {"x": src}).wait_recv()
-    for d in range(1, nn):
-        send(remote(nres.at[n], nres.at[n], ng_s.at[d], ng_r.at[d], {"narrow": at_n(d)}))
-
-    squares = jnp.zeros((rows_n, 1), F32)
-    for k in range(nx):
-        block = nres[n, k].astype(F32)
-        squares = squares + jnp.sum(block * block, axis=1, keepdims=True)
-    r_sub = lax.broadcasted_iota(jnp.int32, (rows_n, rows), 0)
-    r_lane = lax.broadcasted_iota(jnp.int32, (rows_n, rows), 1)
-    zin[z] = jnp.sum(jnp.where(r_lane == r_sub + n * rows_n, squares, 0.0), axis=0, keepdims=True)
-    for d in reversed(by_distance(nz)):
-        send(remote(zin.at[z], zin.at[z], zs_s.at[d], zs_r.at[d], {"z": at_z(d)}))
+    ahead, behind, across = narrow(turn, c), narrow(-turn, c), narrow(2, c)
+    other = narrow(0, 1 - c)
+    send(row_copy(0, n, ahead))
+    send(row_copy(1, n, behind))
+    send(row_copy(3, n, other))
 
     local[3].wait()
     step = kw
@@ -175,23 +188,34 @@
             kc[j, b * step : (b + 1) * step, :] = dot(e0, block).astype(BF16)
             vc[j, b * step : (b + 1) * step, :] = dot(e1, block).astype(BF16)
 
-    for d in range(1, nn):
-        src = at_n(nn - d)
-        remote(nres.at[src], nres.at[src], ng_s.at[d], ng_r.at[d], {"narrow": src}).wait_recv()
+    row_copy(0, behind, behind).wait_recv()
+    send(row_copy(2, behind, ahead))
+    send(row_copy(4, behind, other))
+    row_copy(1, ahead, ahead).wait_recv()
+    send(row_copy(5, ahead, other))
+
+    for d in range(1, nz):
+        src = at_z(nz - d)
+        remote(zin.at[src], zin.at[src], zs_s.at[d], zs_r.at[d], {"z": src}).wait_recv()
+    nsq[x, n] = jnp.sum(zin[...], axis=0)
+    for dx, dn in plane:
+        dev = {"x": at_x(dx), "narrow": at_n(dn)}
+        send(remote(nsq.at[x, n], nsq.at[x, n], ns_s.at[dx, dn], ns_r.at[dx, dn], dev))
+
+    row_copy(2, across, behind).wait_recv()
+    send(row_copy(6, across, other))
+    far = narrow(-2 * turn, 1 - c)
+    for k, src in ((3, other), (4, narrow(turn, 1 - c)), (5, narrow(-turn, 1 - c)), (6, far)):
+        row_copy(k, src, other).wait_recv()
     for k in range(nx):
         block = nres[:, k].reshape(rows, kw)
         sres[:, k * kw : (k + 1) * kw] = dot(pz[...], block).astype(BF16)
 
-    for d in range(1, nz):
-        src = at_z(nz - d)
-        remote(zin.at[src], zin.at[src], zs_s.at[d], zs_r.at[d], {"z": src}).wait_recv()
-    nsq[n] = jnp.sum(zin[...], axis=0)
-    for d in range(1, nn):
-        send(remote(nsq.at[n], nsq.at[n], ns_s.at[d], ns_r.at[d], {"narrow": at_n(d)}))
-    for d in range(1, nn):
-        src = at_n(nn - d)
-        remote(nsq.at[src], nsq.at[src], ns_s.at[d], ns_r.at[d], {"narrow": src}).wait_recv()
-    sums = jnp.sum(nsq[...], axis=0)
+    for dx, dn in plane:
+        src = (at_x(nx - dx), at_n(nn - dn))
+        dev = {"x": src[0], "narrow": src[1]}
+        remote(nsq.at[src], nsq.at[src], ns_s.at[dx, dn], ns_r.at[dx, dn], dev).wait_recv()
+    sums = jnp.sum(nsq[...].reshape(nx * nn, 1, rows), axis=0)
     sum_col = jnp.sum(jnp.where(pz[...].astype(F32) > 0.5, sums, 0.0), axis=1, keepdims=True)
     inverse = lax.rsqrt(sum_col / width + 1e-05)
 
@@ -218,52 +242,44 @@
     total = dot(nrm[:, :kw], wq[0])
     for k in range(1, nx):
         total = total + dot(nrm[:, k * kw : (k + 1) * kw], wq[k])
-    part[:, :, :qcols] = total.reshape(nz, per_z, qcols)
+    for k in range(pieces - 1):
+        part[:, k] = total[:, k * HD : (k + 1) * HD].reshape(nz, per_z, HD)
     half = nrm[:, pl.ds(pl.multiple_of(lax.rem(x, 2) * 2 * kw, 2 * kw), 2 * kw)]
     kv_part = dot(half[:, :kw], kvw[0]) + dot(half[:, kw:], kvw[1])
-    part[:, :, qcols:] = kv_part.reshape(nz, per_z, HD)
+    part[:, pieces - 1] = kv_part.reshape(nz, per_z, HD)
 
     right, left = {"z": at_z(1)}, {"z": at_z(nz - 1)}
     r_steps, l_steps = nz // 2, nz - 1 - nz // 2
-    cols = part.shape[2]
-    cuts = [(0, 384), (384, cols)]
-
-    def r_copy(s, c):
-        lo, hi = cuts[c]
-        owner = at_z(r_steps - s)
-        src = part.at[owner, :, lo:hi] if s == 0 else rbuf.at[s - 1, :, lo:hi]
-        return remote(src, rbuf.at[s, :, lo:hi], rr_s.at[s, c], rr_r.at[s, c], right)
-
-    def l_copy(s, c):
-        lo, hi = cuts[c]
-        owner = at_z(nz - l_steps + s)
-        src = part.at[owner, :, lo:hi] if s == 0 else lbuf.at[s - 1, :, lo:hi]
-        return remote(src, lbuf.at[s, :, lo:hi], lr_s.at[s, c], lr_r.at[s, c], left)
-
-    for c in range(len(cuts)):
-        send(r_copy(0, c))
-        if l_steps > 0:
-            send(l_copy(0, c))
+
+    def r_copy(s, k):
+        src = part.at[at_z(r_steps), k] if s == 0 else rbuf.at[s - 1, k]
+        return remote(src, rbuf.at[s, k], rr_s.at[s, k], rr_r.at[s, k], right)
+
+    def l_copy(s, k):
+        src = part.at[at_z(nz - l_steps), k] if s == 0 else lbuf.at[s - 1, k]
+        return remote(src, lbuf.at[s, k], lr_s.at[s, k], lr_r.at[s, k], left)
+
+    for k in range(pieces):
+        send(r_copy(0, k))
+        send(l_copy(0, k))
     for s in range(r_steps):
-        for c, (lo, hi) in enumerate(cuts):
-            r_copy(s, c).wait_recv()
+        for k in range(pieces):
+            r_copy(s, k).wait_recv()
             if s + 1 < r_steps:
-                owner = at_z(r_steps - s - 1)
-                rbuf[s, :, lo:hi] = rbuf[s, :, lo:hi] + part[owner, :, lo:hi]
-                send(r_copy(s + 1, c))
+                rbuf[s, k] = rbuf[s, k] + part[at_z(r_steps - s - 1), k]
+                send(r_copy(s + 1, k))
+            else:
+                own = part[z, k] + rbuf[s, k] + lbuf[l_steps - 1, k]
+                for t in range(nx):
+                    xs[t, k] = own[t * slots : (t + 1) * slots]
+                for d in range(1, nx):
+                    to = at_x(d)
+                    send(remote(xs.at[to, k], xin.at[x, k], xe_s.at[d, k], xe_r.at[d, k], {"x": to}))
             if s < l_steps:
-                l_copy(s, c).wait_recv()
+                l_copy(s, k).wait_recv()
                 if s + 1 < l_steps:
-                    owner = at_z(nz - l_steps + s + 1)
-                    lbuf[s, :, lo:hi] = lbuf[s, :, lo:hi] + part[owner, :, lo:hi]
-                    send(l_copy(s + 1, c))
-    own = part[z] + rbuf[r_steps - 1]
-    if l_steps > 0:
-        own = own + lbuf[l_steps - 1]
-    for k in range(nx):
-        xs[k] = own[k * slots : (k + 1) * slots]
-    for d in range(1, nx):
-        send(remote(xs.at[at_x(d)], xin.at[x], xe_s.at[d], xe_r.at[d], {"x": at_x(d)}))
+                    lbuf[s, k] = lbuf[s, k] + part[at_z(nz - l_steps + s + 1), k]
+                    send(l_copy(s + 1, k))
     xin[x] = xs[x]
 
     local[5].wait()
@@ -277,16 +293,17 @@
     def rotate(v):
         return (v * cosine + pltpu.roll(v, HD // 2, 1) * sine).astype(BF16).astype(F32)
 
-    for d in range(1, nx):
-        src = at_x(nx - d)
-        remote(xs.at[0], xin.at[src], xe_s.at[d], xe_r.at[d], {"x": src}).wait_recv()
+    for k in range(pieces):
+        for d in range(1, nx):
+            src = at_x(nx - d)
+            remote(xs.at[0, k], xin.at[src, k], xe_s.at[d, k], xe_r.at[d, k], {"x": src}).wait_recv()
     for k in range(nx):
         for i in range(heads_x):
-            turned_query = rotate(xin[k, :, i * HD : (i + 1) * HD])
+            turned_query = rotate(xin[k, i])
             for j in range(slots):
                 q_ref[j, k * heads_x + i : k * heads_x + i + 1, :] = turned_query[j : j + 1]
-    keys_new = rotate(xin[0, :, qcols:] + xin[1, :, qcols:])
-    values_new = (xin[2, :, qcols:] + xin[3, :, qcols:]).astype(BF16).astype(F32)
+    keys_new = rotate(xin[0, pieces - 1] + xin[1, pieces - 1])
+    values_new = (xin[2, pieces - 1] + xin[3, pieces - 1]).astype(BF16).astype(F32)
 
     scale = 1.0 / math.sqrt(HD)
     position = lax.broadcasted_iota(jnp.int32, (heads, most), 1)
@@ -306,26 +323,51 @@
             ab[j : j + 1, h * HD : (h + 1) * HD] = attended[h : h + 1]
     ag[w_own] = ab[...].astype(BF16)
 
-    for d in reversed(by_distance(nz)):
-        send(remote(ag.at[w_own], ag.at[w_own], az_s.at[d], az_r.at[d], {"z": at_z(d)}))
-    for d in [0] + by_distance(nz):
-        src_z = at_z(nz - d)
-        block = x * nz + src_z
-        if d > 0:
-            remote(ag.at[block], ag.at[block], az_s.at[d], az_r.at[d], {"z": src_z}).wait_recv()
-        for e in range(1, nx):
-            send(remote(ag.at[block], ag.at[block], ax_s.at[d, e], ax_r.at[d, e], {"x": at_x(e)}))
+    reach = nz // 4
+
+    def z_copy(d, block, to):
+        return remote(ag.at[block], ag.at[block], az_s.at[d], az_r.at[d], {"z": to})
+
+    def x_copy(d, e, block, to):
+        return remote(ag.at[block], ag.at[block], ax_s.at[d, e], ax_r.at[d, e], {"x": to})
+
+    def block_of(e, d):
+        return at_x(nx - e) * nz + at_z(nz - d)
+
+    for k in range(reach, 0, -1):
+        send(z_copy(k, w_own, at_z(k)))
+        send(z_copy(nz - k, w_own, at_z(nz - k)))
+    order = [0] + by_distance(nz)
+    lag = 4
+    for step in range(len(order) + lag):
+        if step < len(order):
+            d = order[step]
+            block = block_of(0, d)
+            if d > 0:
+                z_copy(d, block, z).wait_recv()
+            if d == reach:
+                for k in range(1, reach + 1):
+                    send(z_copy(reach + k, block, at_z(k)))
+            if d == nz - reach:
+                for k in range(1, reach):
+                    send(z_copy(nz - reach - k, block, at_z(nz - k)))
+            send(x_copy(d, 1, block, at_x(1)))
+            send(x_copy(d, nx - 1, block, at_x(nx - 1)))
+        if step >= lag:
+            d = order[step - lag]
+            e = 1 if d % 2 == 0 else nx - 1
+            block = block_of(e, d)
+            x_copy(d, e, block, x).wait_recv()
+            send(x_copy(d, 2, block, at_x(e)))
     local[4].wait()
-    for d in [0] + by_distance(nz):
-        for e in range(1, nx):
-            src_x = at_x(nx - e)
-            block = src_x * nz + at_z(nz - d)
-            remote(ag.at[block], ag.at[block], ax_s.at[d, e], ax_r.at[d, e], {"x": src_x}).wait_recv()
+    for d in order:
+        for e in (nx - 1 if d % 2 == 0 else 1, 2):
+            x_copy(d, e, block_of(e, d), x).wait_recv()
 
     group = 16 // slots
     for g in range(rows // 16):
-        pieces = [ag[g * group + i].astype(F32) for i in range(group)]
-        att[g * 16 : (g + 1) * 16, :] = jnp.concatenate(pieces, axis=0).astype(BF16)
+        blocks = [ag[g * group + i].astype(F32) for i in range(group)]
+        att[g * 16 : (g + 1) * 16, :] = jnp.concatenate(blocks, axis=0).astype(BF16)
     tile = 512
     update = jnp.zeros((rows, wo.shape[1]), F32)
     for k in range(att.shape[1] // tile):
@@ -361,7 +403,7 @@
     rows_n = residual.shape[0]
     rows = rows_n * nn
     qcols = query_cols // nx
-    cols = qcols + HD
+    pieces = qcols // HD + 1
     heads = query_cols // HD
     r_steps, l_steps = nz // 2, max(nz - 1 - nz // 2, 1)
     width = kw * nx * nz
@@ -381,38 +423,39 @@
         pltpu.VMEM((slots, most, HD), BF16),
         pltpu.VMEM((slots, most, HD), BF16),
         pltpu.VMEM(table.shape, F32),
+        pltpu.VMEM((kw,), BF16),
         pltpu.VMEM((nz, 1, rows), F32),
-        pltpu.VMEM((nn, 1, rows), F32),
+        pltpu.VMEM((nx, nn, 1, rows), F32),
         pltpu.VMEM((rows, rows), BF16),
         pltpu.VMEM((rows, rows), BF16),
         pltpu.VMEM((rows, nx * kw), BF16),
         pltpu.VMEM((rows, nx * kw), BF16),
-        pltpu.VMEM((nz, nx * slots, cols), F32),
-        pltpu.VMEM((r_steps, nx * slots, cols), F32),
-        pltpu.VMEM((l_steps, nx * slots, cols), F32),
-        pltpu.VMEM((nx, slots, cols), F32),
-        pltpu.VMEM((nx, slots, cols), F32),
+        pltpu.VMEM((nz, pieces, nx * slots, HD), F32),
+        pltpu.VMEM((r_steps, pieces, nx * slots, HD), F32),
+        pltpu.VMEM((l_steps, pieces, nx * slots, HD), F32),
+        pltpu.VMEM((nx, pieces, slots, HD), F32),
+        pltpu.VMEM((nx, pieces, slots, HD), F32),
         pltpu.VMEM((slots, heads, HD), F32),
         pltpu.VMEM((slots, query_cols), F32),
         pltpu.VMEM((nx * nz, slots, query_cols), BF16),
         pltpu.VMEM((rows, query_cols), BF16),
         pltpu.VMEM((nn, rows_n, w_out.shape[1]), F32),
         pltpu.VMEM((nn, rows_n, w_out.shape[1]), F32),
-        dma((6,)),
+        dma((7,)),
         dma((nx,)), dma((nx,)), dma((nx,)), dma((nx,)), dma((nx,)), dma((nx,)),
         dma((2,)), dma((2,)),
-        dma((nn,)), dma((nn,)),
+        dma((7,)), dma((7,)),
         dma((nz,)), dma((nz,)),
-        dma((nn,)), dma((nn,)),
-        dma((r_steps, 2)), dma((r_steps, 2)), dma((l_steps, 2)), dma((l_steps, 2)),
-        dma((nx,)), dma((nx,)),
+        dma((nx, nn)), dma((nx, nn)),
+        dma((r_steps, pieces)), dma((r_steps, pieces)), dma((l_steps, pieces)), dma((l_steps, pieces)),
+        dma((nx, pieces)), dma((nx, pieces)),
         dma((nz,)), dma((nz,)), dma((nz, nx)), dma((nz, nx)),
         dma((nn,)), dma((nn,)),
     ]
     return pl.pallas_call(
         functools.partial(kernel, nx, nz, nn, width),
         out_shape=jax.ShapeDtypeStruct(residual.shape, BF16),
-        in_specs=[smem, smem, anywhere, vmem, vmem] + [anywhere] * 5,
+        in_specs=[smem, smem, anywhere, anywhere, vmem] + [anywhere] * 5,
         out_specs=vmem,
         scratch_shapes=scratch,
         compiler_params=pltpu.CompilerParams(
@@ -423,7 +466,7 @@
         lengths,
         assignment,
         residual,
-        norm_gain.reshape(1, -1),
+        norm_gain,
         assignment.reshape(1, -1),
         w_query,
         w_keyval.reshape(2 * kw, channels),

time: 95.5 us -> 101 us (1.058)
  Pallas kernels: 92.7 us -> 99.7 us
  local copies, waits for them, and re-layouts: 2.54 us -> 1.32 us
    pallas_call x1, Pallas kernels: 92.7 us -> 99.7 us  [per_device(): pl.pallas_call(functools.partial(kernel, nx, nz, nn, width), out_shape=ja...]
    reshape x1 -> x0, local copies, waits for them, and re-layouts: 1.22 us -> none  [per_device(): norm_gain.reshape(1, -1)]
where the time goes in v2:
time: 101 us
  Pallas kernels  99.7 us (99%)
  local copies, waits for them, and re-layouts  1.32 us (1%)
    pallas_call x1, Pallas kernels, per_device(): pl.pallas_call(functools.partial(kernel, nx, nz, nn, width), out_shape=ja...  99.7 us

profile of v2, /device:TPU:1, one launch (start us, length us, event | category | flops | bytes accessed | tf_op | source)
XLA Modules:
  0.0 101.0 jit_solution(712224385713807243)
XLA Ops:
  0.0 99.7 %decode_block.1 = bf16[32,256]{1,0:T(8,128)(2,1)} custom-call(s32[256]{0:T(256)} %lens.1, s32[256]{0:T(256)} %asg.1, bf16[32,256]{1,0:T(8,128)(2,1)} %res_h.1, bf16[256]{0:T(256)(128)(2,1)} %gain_h.1, s32[1,256]{1,0:T(1,128)} %bitcast.5, bf16[256,2048]{1,0:T(8,128)(2,1)} %wq_h.1, bf16[512,128]{1,0:T(8,128)(2,1)} %bitcast.4, bf16[2048,256]{1,0:T(8,128)(2,1)} %wo_h.1, ...), custom_call_target="tpu_custom_call" | custom-call | tf_op jit(solution)/shard_map/decode_block/pallas_call | solution.py:455
  99.7 1.3 %copy.11 = bf16[32,256]{1,0:T(8,128)(2,1)} copy(bf16[32,256]{1,0:T(8,128)(2,1)} %decode_block.1) | data formatting | bytes 32768

commit v3 on v1

--- a/solution.py
+++ b/solution.py
@@ -40,19 +40,23 @@
 
 def kernel(
     nx, nz, nn, width,
-    lens, asg, res_h, gain_ref, asg_ref, wq_h, wkv_h, wo_h, cache_h, tab_h,
+    lens, asg, res_h, gain_h, asg_ref, wq_h, wkv_h, wo_h, cache_h, tab_h,
     out_ref,
     nres, gains, wq, wkv, kvs, kvw, wo, cache, kc, vc, tab,
-    zin, nsq, pz, pr, sres, nrm, part, rbuf, lbuf, xs, xin, q_ref, ab, ag, att, nst, nin,
+    gain_v, zin, nsq, pz, pr, sres, nrm, part, r_even, r_odd, l_even, l_odd, wrel, xs, xin, q_ref, ab, ag, att, nst, nin,
     loc, xr_s, xr_r, xg_s, xg_r, xw_s, xw_r, kv_s, kv_r, ng_s, ng_r,
-    zs_s, zs_r, ns_s, ns_r, rr_s, rr_r, lr_s, lr_r, xe_s, xe_r,
+    zs_s, zs_r, ns_s, ns_r, re_s, re_r, ro_s, ro_r, le_s, le_r, lo_s, lo_r, wr_s, wr_r, wf_s, wf_r, xe_s, xe_r,
     az_s, az_r, ax_s, ax_r, no_s, no_r,
 ):
     x, z, n = lax.axis_index("x"), lax.axis_index("z"), lax.axis_index("narrow")
+    y, c = n // 2, n % 2
+    ny = nn // 2
+    turn = 1 - 2 * c
     rows = pz.shape[0]
     rows_n = rows // nn
-    slots = xs.shape[1]
+    slots = xs.shape[2]
     per_z = nx * slots
+    pieces = part.shape[1]
     qcols = wq.shape[2]
     kw = wq.shape[1]
     most = kc.shape[1]
@@ -78,6 +82,7 @@
         return wq_h.at[:, pl.ds(pl.multiple_of(t * qcols, qcols), qcols)]
 
     local = [
+        pltpu.make_async_copy(gain_h, gain_v, loc.at[6]),
         pltpu.make_async_copy(wkv_h, wkv, loc.at[0]),
         pltpu.make_async_copy(res_h, nres.at[n, x], loc.at[1]),
         pltpu.make_async_copy(wq_part(x), wq.at[x], loc.at[2]),
@@ -94,6 +99,33 @@
         pl.semaphore_signal(barrier, inc=1, device_id={"narrow": at_n(d)}, device_id_type=MESH)
     for copy in local:
         copy.start()
+    gain_in, wkv_in, res_in, wq_in, cache_in, wo_in, tab_in = local
+    pl.semaphore_wait(barrier, (nx - 1) + (nz - 1) + (nn - 1))
+
+    sends = []
+
+    def send(copy):
+        copy.start()
+        sends.append(copy)
+
+    def relay_half(i, src, to):
+        return remote(src, wrel.at[i], wr_s.at[i], wr_r.at[i], {"x": to})
+
+    def relayed(i, owner, to):
+        half = wq.at[owner, i * (kw // 2) : (i + 1) * (kw // 2)]
+        return remote(wrel.at[i], half, wf_s.at[i], wf_r.at[i], {"x": to})
+
+    for d in range(1, nx):
+        send(remote(res_h, nres.at[n, x], xr_s.at[d], xr_r.at[d], {"x": at_x(d)}))
+    gain_in.wait()
+    gains[x] = gain_v[...].astype(F32).reshape(1, kw)
+    for d in range(1, nx):
+        send(remote(gains.at[x], gains.at[x], xg_s.at[d], xg_r.at[d], {"x": at_x(d)}))
+    far_cols = pl.ds(pl.multiple_of(at_x(2) * qcols, qcols), qcols)
+    send(relay_half(0, wq_h.at[0 : kw // 2, far_cols], at_x(1)))
+    send(relay_half(1, wq_h.at[kw // 2 : kw, far_cols], at_x(nx - 1)))
+    for d in (1, nx - 1):
+        send(remote(wq_part(at_x(d)), wq.at[x], xw_s.at[d], xw_r.at[d], {"x": at_x(d)}))
 
     a_row = asg_ref[...]
     i_sub = lax.broadcasted_iota(jnp.int32, (rows, rows), 0)
@@ -106,30 +138,15 @@
     pick = i_lane == a_col
     pz[...] = jnp.where(pick, 1.0, 0.0).astype(BF16)
     pr[...] = jnp.where(i_sub == a_row, 1.0, 0.0).astype(BF16)
-    gains[x] = gain_ref[...].astype(F32)
 
     e_row = lax.broadcasted_iota(jnp.int32, (kw, 2 * kw), 0)
     e_col = lax.broadcasted_iota(jnp.int32, (kw, 2 * kw), 1)
     e0 = jnp.where(e_col == 2 * e_row, 1.0, 0.0).astype(BF16)
     e1 = jnp.where(e_col == 2 * e_row + 1, 1.0, 0.0).astype(BF16)
-    local[0].wait()
+    wkv_in.wait()
     kvs[0] = dot(e0, wkv[...]).astype(BF16)
     kvs[1] = dot(e1, wkv[...]).astype(BF16)
 
-    pl.semaphore_wait(barrier, (nx - 1) + (nz - 1) + (nn - 1))
-
-    sends = []
-
-    def send(copy):
-        copy.start()
-        sends.append(copy)
-
-    for d in range(1, nx):
-        dev = {"x": at_x(d)}
-        send(remote(res_h, nres.at[n, x], xr_s.at[d], xr_r.at[d], dev))
-        send(remote(gains.at[x], gains.at[x], xg_s.at[d], xg_r.at[d], dev))
-    for d in range(1, nx):
-        send(remote(wq_part(at_x(d)), wq.at[x], xw_s.at[d], xw_r.at[d], {"x": at_x(d)}))
     kv_slot = lax.rem(x, 2)
     k_copy = remote(kvs.at[0], kvw.at[kv_slot], kv_s.at[0], kv_r.at[kv_slot], {"x": x // 2})
     v_copy = remote(kvs.at[1], kvw.at[kv_slot], kv_s.at[1], kv_r.at[kv_slot], {"x": 2 + x // 2})
@@ -150,12 +167,21 @@
     def _():
         kvw[1] = kvs[1]
 
-    local[1].wait()
+    def narrow(dy, core):
+        return lax.rem(y + dy + ny, ny) * 2 + core
+
+    def row_copy(k, src, to):
+        return remote(nres.at[src], nres.at[src], ng_s.at[k], ng_r.at[k], {"narrow": to})
+
+    res_in.wait()
     for d in range(1, nx):
         src = at_x(nx - d)
         remote(res_h, nres.at[n, src], xr_s.at[d], xr_r.at[d], {"x": src}).wait_recv()
-    for d in range(1, nn):
-        send(remote(nres.at[n], nres.at[n], ng_s.at[d], ng_r.at[d], {"narrow": at_n(d)}))
+    ahead, behind, across = narrow(turn, c), narrow(-turn, c), narrow(2, c)
+    other = narrow(0, 1 - c)
+    send(row_copy(0, n, ahead))
+    send(row_copy(1, n, behind))
+    send(row_copy(3, n, other))
 
     squares = jnp.zeros((rows_n, 1), F32)
     for k in range(nx):
@@ -167,7 +193,7 @@
     for d in reversed(by_distance(nz)):
         send(remote(zin.at[z], zin.at[z], zs_s.at[d], zs_r.at[d], {"z": at_z(d)}))
 
-    local[3].wait()
+    cache_in.wait()
     step = kw
     for j in range(slots):
         for b in range(most // step):
@@ -175,12 +201,19 @@
             kc[j, b * step : (b + 1) * step, :] = dot(e0, block).astype(BF16)
             vc[j, b * step : (b + 1) * step, :] = dot(e1, block).astype(BF16)
 
-    for d in range(1, nn):
-        src = at_n(nn - d)
-        remote(nres.at[src], nres.at[src], ng_s.at[d], ng_r.at[d], {"narrow": src}).wait_recv()
-    for k in range(nx):
-        block = nres[:, k].reshape(rows, kw)
-        sres[:, k * kw : (k + 1) * kw] = dot(pz[...], block).astype(BF16)
+    left_x, right_x, opposite = at_x(nx - 1), at_x(1), at_x(2)
+    relay_half(0, wrel.at[0], left_x).wait_recv()
+    send(relayed(0, left_x, right_x))
+    relay_half(1, wrel.at[1], right_x).wait_recv()
+    send(relayed(1, right_x, left_x))
+
+    row_copy(0, behind, behind).wait_recv()
+    send(row_copy(2, behind, ahead))
+    send(row_copy(4, behind, other))
+    row_copy(1, ahead, ahead).wait_recv()
+    send(row_copy(5, ahead, other))
+    row_copy(2, across, behind).wait_recv()
+    send(row_copy(6, across, other))
 
     for d in range(1, nz):
         src = at_z(nz - d)
@@ -188,6 +221,14 @@
     nsq[n] = jnp.sum(zin[...], axis=0)
     for d in range(1, nn):
         send(remote(nsq.at[n], nsq.at[n], ns_s.at[d], ns_r.at[d], {"narrow": at_n(d)}))
+
+    far = narrow(-2 * turn, 1 - c)
+    for k, src in ((3, other), (4, narrow(turn, 1 - c)), (5, narrow(-turn, 1 - c)), (6, far)):
+        row_copy(k, src, other).wait_recv()
+    for k in range(nx):
+        block = nres[:, k].reshape(rows, kw)
+        sres[:, k * kw : (k + 1) * kw] = dot(pz[...], block).astype(BF16)
+
     for d in range(1, nn):
         src = at_n(nn - d)
         remote(nsq.at[src], nsq.at[src], ns_s.at[d], ns_r.at[d], {"narrow": src}).wait_recv()
@@ -202,10 +243,12 @@
         block = sres[:, k * kw : (k + 1) * kw].astype(F32)
         nrm[:, k * kw : (k + 1) * kw] = (block * inverse * gains[k]).astype(BF16)
 
-    local[2].wait()
-    for d in range(1, nx):
+    wq_in.wait()
+    for d in (1, nx - 1):
         src = at_x(nx - d)
         remote(wq_part(src), wq.at[src], xw_s.at[d], xw_r.at[d], {"x": src}).wait_recv()
+    relayed(0, opposite, left_x).wait_recv()
+    relayed(1, opposite, right_x).wait_recv()
 
     @pl.when(x != 0)
     def _():
@@ -218,55 +261,66 @@
     total = dot(nrm[:, :kw], wq[0])
     for k in range(1, nx):
         total = total + dot(nrm[:, k * kw : (k + 1) * kw], wq[k])
-    part[:, :, :qcols] = total.reshape(nz, per_z, qcols)
+    for k in range(pieces - 1):
+        part[:, k] = total[:, k * HD : (k + 1) * HD].reshape(nz, per_z, HD)
     half = nrm[:, pl.ds(pl.multiple_of(lax.rem(x, 2) * 2 * kw, 2 * kw), 2 * kw)]
     kv_part = dot(half[:, :kw], kvw[0]) + dot(half[:, kw:], kvw[1])
-    part[:, :, qcols:] = kv_part.reshape(nz, per_z, HD)
-
-    right, left = {"z": at_z(1)}, {"z": at_z(nz - 1)}
-    r_steps, l_steps = nz // 2, nz - 1 - nz // 2
-    cols = part.shape[2]
-    cuts = [(0, 384), (384, cols)]
-
-    def r_copy(s, c):
-        lo, hi = cuts[c]
-        owner = at_z(r_steps - s)
-        src = part.at[owner, :, lo:hi] if s == 0 else rbuf.at[s - 1, :, lo:hi]
-        return remote(src, rbuf.at[s, :, lo:hi], rr_s.at[s, c], rr_r.at[s, c], right)
-
-    def l_copy(s, c):
-        lo, hi = cuts[c]
-        owner = at_z(nz - l_steps + s)
-        src = part.at[owner, :, lo:hi] if s == 0 else lbuf.at[s - 1, :, lo:hi]
-        return remote(src, lbuf.at[s, :, lo:hi], lr_s.at[s, c], lr_r.at[s, c], left)
-
-    for c in range(len(cuts)):
-        send(r_copy(0, c))
-        if l_steps > 0:
-            send(l_copy(0, c))
-    for s in range(r_steps):
-        for c, (lo, hi) in enumerate(cuts):
-            r_copy(s, c).wait_recv()
-            if s + 1 < r_steps:
-                owner = at_z(r_steps - s - 1)
-                rbuf[s, :, lo:hi] = rbuf[s, :, lo:hi] + part[owner, :, lo:hi]
-                send(r_copy(s + 1, c))
-            if s < l_steps:
-                l_copy(s, c).wait_recv()
-                if s + 1 < l_steps:
-                    owner = at_z(nz - l_steps + s + 1)
-                    lbuf[s, :, lo:hi] = lbuf[s, :, lo:hi] + part[owner, :, lo:hi]
-                    send(l_copy(s + 1, c))
-    own = part[z] + rbuf[r_steps - 1]
-    if l_steps > 0:
-        own = own + lbuf[l_steps - 1]
-    for k in range(nx):
-        xs[k] = own[k * slots : (k + 1) * slots]
-    for d in range(1, nx):
-        send(remote(xs.at[at_x(d)], xin.at[x], xe_s.at[d], xe_r.at[d], {"x": at_x(d)}))
+    part[:, pieces - 1] = kv_part.reshape(nz, per_z, HD)
+
+    steps = nz // 4
+    sides = ((1, r_even, r_odd, re_s, re_r, ro_s, ro_r), (-1, l_even, l_odd, le_s, le_r, lo_s, lo_r))
+
+    def along(side, d):
+        return at_z(d if side[0] > 0 else nz - d)
+
+    def odd_copy(side, i, k):
+        src = part.at[along(side, 2 * i + 1), k]
+        to = {"z": along(side, 1)}
+        return remote(src, side[2].at[i, k], side[5].at[i, k], side[6].at[i, k], to)
+
+    def even_copy(side, s, k):
+        if s == 0:
+            src = part.at[along(side, 2 * steps), k]
+        elif s == 1 and side[0] < 0:
+            src = side[2].at[steps - 1, k]
+        else:
+            src = side[1].at[s - 1, k]
+        to = {"z": along(side, 2)}
+        return remote(src, side[1].at[s, k], side[3].at[s, k], side[4].at[s, k], to)
+
+    for k in range(pieces):
+        send(even_copy(sides[0], 0, k))
+        for side in sides:
+            send(odd_copy(side, steps - 1, k))
+    for i in range(steps - 2, -1, -1):
+        for k in range(pieces):
+            for side in sides:
+                send(odd_copy(side, i, k))
+    for s in range(1, steps):
+        for k in range(pieces):
+            for side in sides:
+                own_part = part[along(side, 2 * (steps - s)), k]
+                odd_copy(side, steps - s, k).wait_recv()
+                if s == 1 and side[0] < 0:
+                    side[2][steps - 1, k] = side[2][steps - 1, k] + own_part
+                else:
+                    even_copy(side, s - 1, k).wait_recv()
+                    side[1][s - 1, k] = side[1][s - 1, k] + side[2][steps - s, k] + own_part
+                send(even_copy(side, s, k))
+    for k in range(pieces):
+        own = part[z, k]
+        for side in sides:
+            odd_copy(side, 0, k).wait_recv()
+            even_copy(side, steps - 1, k).wait_recv()
+            own = own + side[1][steps - 1, k] + side[2][0, k]
+        for t in range(nx):
+            xs[t, k] = own[t * slots : (t + 1) * slots]
+        for d in range(1, nx):
+            to = at_x(d)
+            send(remote(xs.at[to, k], xin.at[x, k], xe_s.at[d, k], xe_r.at[d, k], {"x": to}))
     xin[x] = xs[x]
 
-    local[5].wait()
+    tab_in.wait()
     lengths = [lens[asg[w_own * slots + j]] for j in range(slots)]
     angles = jnp.concatenate([tab[pl.ds(lengths[j], 1), :] for j in range(slots)], axis=0)
     turned = pltpu.roll(angles, HD // 2, 1)
@@ -277,16 +331,17 @@
     def rotate(v):
         return (v * cosine + pltpu.roll(v, HD // 2, 1) * sine).astype(BF16).astype(F32)
 
-    for d in range(1, nx):
-        src = at_x(nx - d)
-        remote(xs.at[0], xin.at[src], xe_s.at[d], xe_r.at[d], {"x": src}).wait_recv()
+    for k in range(pieces):
+        for d in range(1, nx):
+            src = at_x(nx - d)
+            remote(xs.at[0, k], xin.at[src, k], xe_s.at[d, k], xe_r.at[d, k], {"x": src}).wait_recv()
     for k in range(nx):
         for i in range(heads_x):
-            turned_query = rotate(xin[k, :, i * HD : (i + 1) * HD])
+            turned_query = rotate(xin[k, i])
             for j in range(slots):
                 q_ref[j, k * heads_x + i : k * heads_x + i + 1, :] = turned_query[j : j + 1]
-    keys_new = rotate(xin[0, :, qcols:] + xin[1, :, qcols:])
-    values_new = (xin[2, :, qcols:] + xin[3, :, qcols:]).astype(BF16).astype(F32)
+    keys_new = rotate(xin[0, pieces - 1] + xin[1, pieces - 1])
+    values_new = (xin[2, pieces - 1] + xin[3, pieces - 1]).astype(BF16).astype(F32)
 
     scale = 1.0 / math.sqrt(HD)
     position = lax.broadcasted_iota(jnp.int32, (heads, most), 1)
@@ -315,7 +370,7 @@
             remote(ag.at[block], ag.at[block], az_s.at[d], az_r.at[d], {"z": src_z}).wait_recv()
         for e in range(1, nx):
             send(remote(ag.at[block], ag.at[block], ax_s.at[d, e], ax_r.at[d, e], {"x": at_x(e)}))
-    local[4].wait()
+    wo_in.wait()
     for d in [0] + by_distance(nz):
         for e in range(1, nx):
             src_x = at_x(nx - e)
@@ -324,8 +379,8 @@
 
     group = 16 // slots
     for g in range(rows // 16):
-        pieces = [ag[g * group + i].astype(F32) for i in range(group)]
-        att[g * 16 : (g + 1) * 16, :] = jnp.concatenate(pieces, axis=0).astype(BF16)
+        blocks = [ag[g * group + i].astype(F32) for i in range(group)]
+        att[g * 16 : (g + 1) * 16, :] = jnp.concatenate(blocks, axis=0).astype(BF16)
     tile = 512
     update = jnp.zeros((rows, wo.shape[1]), F32)
     for k in range(att.shape[1] // tile):
@@ -361,9 +416,9 @@
     rows_n = residual.shape[0]
     rows = rows_n * nn
     qcols = query_cols // nx
-    cols = qcols + HD
+    pieces = qcols // HD + 1
     heads = query_cols // HD
-    r_steps, l_steps = nz // 2, max(nz - 1 - nz // 2, 1)
+    steps = nz // 4
     width = kw * nx * nz
     anywhere = pl.BlockSpec(memory_space=pl.ANY)
     vmem = pl.BlockSpec(memory_space=pltpu.VMEM)
@@ -381,38 +436,43 @@
         pltpu.VMEM((slots, most, HD), BF16),
         pltpu.VMEM((slots, most, HD), BF16),
         pltpu.VMEM(table.shape, F32),
+        pltpu.VMEM((kw,), BF16),
         pltpu.VMEM((nz, 1, rows), F32),
         pltpu.VMEM((nn, 1, rows), F32),
         pltpu.VMEM((rows, rows), BF16),
         pltpu.VMEM((rows, rows), BF16),
         pltpu.VMEM((rows, nx * kw), BF16),
         pltpu.VMEM((rows, nx * kw), BF16),
-        pltpu.VMEM((nz, nx * slots, cols), F32),
-        pltpu.VMEM((r_steps, nx * slots, cols), F32),
-        pltpu.VMEM((l_steps, nx * slots, cols), F32),
-        pltpu.VMEM((nx, slots, cols), F32),
-        pltpu.VMEM((nx, slots, cols), F32),
+        pltpu.VMEM((nz, pieces, nx * slots, HD), F32),
+        pltpu.VMEM((steps, pieces, nx * slots, HD), F32),
+        pltpu.VMEM((steps, pieces, nx * slots, HD), F32),
+        pltpu.VMEM((steps, pieces, nx * slots, HD), F32),
+        pltpu.VMEM((steps, pieces, nx * slots, HD), F32),
+        pltpu.VMEM((2, kw // 2, qcols), BF16),
+        pltpu.VMEM((nx, pieces, slots, HD), F32),
+        pltpu.VMEM((nx, pieces, slots, HD), F32),
         pltpu.VMEM((slots, heads, HD), F32),
         pltpu.VMEM((slots, query_cols), F32),
         pltpu.VMEM((nx * nz, slots, query_cols), BF16),
         pltpu.VMEM((rows, query_cols), BF16),
         pltpu.VMEM((nn, rows_n, w_out.shape[1]), F32),
         pltpu.VMEM((nn, rows_n, w_out.shape[1]), F32),
-        dma((6,)),
+        dma((7,)),
         dma((nx,)), dma((nx,)), dma((nx,)), dma((nx,)), dma((nx,)), dma((nx,)),
         dma((2,)), dma((2,)),
-        dma((nn,)), dma((nn,)),
+        dma((7,)), dma((7,)),
         dma((nz,)), dma((nz,)),
         dma((nn,)), dma((nn,)),
-        dma((r_steps, 2)), dma((r_steps, 2)), dma((l_steps, 2)), dma((l_steps, 2)),
-        dma((nx,)), dma((nx,)),
+        *[dma((steps, pieces))] * 8,
+        dma((2,)), dma((2,)), dma((2,)), dma((2,)),
+        dma((nx, pieces)), dma((nx, pieces)),
         dma((nz,)), dma((nz,)), dma((nz, nx)), dma((nz, nx)),
         dma((nn,)), dma((nn,)),
     ]
     return pl.pallas_call(
         functools.partial(kernel, nx, nz, nn, width),
         out_shape=jax.ShapeDtypeStruct(residual.shape, BF16),
-        in_specs=[smem, smem, anywhere, vmem, vmem] + [anywhere] * 5,
+        in_specs=[smem, smem, anywhere, anywhere, vmem] + [anywhere] * 5,
         out_specs=vmem,
         scratch_shapes=scratch,
         compiler_params=pltpu.CompilerParams(
@@ -423,7 +483,7 @@
         lengths,
         assignment,
         residual,
-        norm_gain.reshape(1, -1),
+        norm_gain,
         assignment.reshape(1, -1),
         w_query,
         w_keyval.reshape(2 * kw, channels),

time: 95.5 us -> 88.7 us (0.929)
  Pallas kernels: 92.7 us -> 87.1 us
  local copies, waits for them, and re-layouts: 2.54 us -> 1.32 us
    pallas_call x1, Pallas kernels: 92.7 us -> 87.1 us  [per_device(): pl.pallas_call(functools.partial(kernel, nx, nz, nn, width), out_shape=ja...]
    reshape x1 -> x0, local copies, waits for them, and re-layouts: 1.22 us -> none  [per_device(): norm_gain.reshape(1, -1)]
where the time goes in v3:
time: 88.7 us; the launch traced here: 88.5 us
  Pallas kernels  87.1 us (98%)
  local copies, waits for them, and re-layouts  1.32 us (1%)
    pallas_call x1, Pallas kernels, per_device(): pl.pallas_call(functools.partial(kernel, nx, nz, nn, width), out_shape=ja...  87.1 us

profile of v3, /device:TPU:1, one launch (start us, length us, event | category | flops | bytes accessed | tf_op | source)
XLA Modules:
  0.0 88.5 jit_solution(2354096581439150958)
XLA Ops:
  0.0 87.1 %decode_block.1 = bf16[32,256]{1,0:T(8,128)(2,1)} custom-call(s32[256]{0:T(256)} %lens.1, s32[256]{0:T(256)} %asg.1, bf16[32,256]{1,0:T(8,128)(2,1)} %res_h.1, bf16[256]{0:T(256)(128)(2,1)} %gain_h.1, s32[1,256]{1,0:T(1,128)} %bitcast.5, bf16[256,2048]{1,0:T(8,128)(2,1)} %wq_h.1, bf16[512,128]{1,0:T(8,128)(2,1)} %bitcast.4, bf16[2048,256]{1,0:T(8,128)(2,1)} %wo_h.1, ...), custom_call_target="tpu_custom_call" | custom-call | tf_op jit(solution)/shard_map/decode_block/pallas_call | solution.py:472
  87.1 1.3 %copy.11 = bf16[32,256]{1,0:T(8,128)(2,1)} copy(bf16[32,256]{1,0:T(8,128)(2,1)} %decode_block.1) | data formatting | bytes 32768

commit v4 on v3

--- a/solution.py
+++ b/solution.py
@@ -43,7 +43,7 @@
     lens, asg, res_h, gain_h, asg_ref, wq_h, wkv_h, wo_h, cache_h, tab_h,
     out_ref,
     nres, gains, wq, wkv, kvs, kvw, wo, cache, kc, vc, tab,
-    gain_v, zin, nsq, pz, pr, sres, nrm, part, r_even, r_odd, l_even, l_odd, wrel, xs, xin, q_ref, ab, ag, att, nst, nin,
+    gain_v, zin, nsq, pz, pr, sres, nrm, part, r_even, r_odd, l_even, l_odd, wrel, xs, xin, q_ref, ab, ag, att, mine, nst, nin,
     loc, xr_s, xr_r, xg_s, xg_r, xw_s, xw_r, kv_s, kv_r, ng_s, ng_r,
     zs_s, zs_r, ns_s, ns_r, re_s, re_r, ro_s, ro_r, le_s, le_r, lo_s, lo_r, wr_s, wr_r, wf_s, wf_r, xe_s, xe_r,
     az_s, az_r, ax_s, ax_r, no_s, no_r,
@@ -361,21 +361,53 @@
             ab[j : j + 1, h * HD : (h + 1) * HD] = attended[h : h + 1]
     ag[w_own] = ab[...].astype(BF16)
 
-    for d in reversed(by_distance(nz)):
-        send(remote(ag.at[w_own], ag.at[w_own], az_s.at[d], az_r.at[d], {"z": at_z(d)}))
-    for d in [0] + by_distance(nz):
-        src_z = at_z(nz - d)
-        block = x * nz + src_z
-        if d > 0:
-            remote(ag.at[block], ag.at[block], az_s.at[d], az_r.at[d], {"z": src_z}).wait_recv()
+    reach = nz // 4
+
+    def z_copy(d, block, to):
+        return remote(ag.at[block], ag.at[block], az_s.at[d], az_r.at[d], {"z": to})
+
+    def x_copy(d, e, block, to):
+        return remote(ag.at[block], ag.at[block], ax_s.at[d, e], ax_r.at[d, e], {"x": to})
+
+    def block_of(e, d):
+        return at_x(nx - e) * nz + at_z(nz - d)
+
+    def along_x(d, hops):
+        for e in hops:
+            send(x_copy(d, e, block_of(0, d), at_x(e)))
+
+    for k in range(reach, 0, -1):
+        send(z_copy(k, w_own, at_z(k)))
+        send(z_copy(nz - k, w_own, at_z(nz - k)))
+    order = [0] + by_distance(nz)
+    near = [d for d in order if min(d, nz - d) <= reach]
+    far = [d for d in order if min(d, nz - d) > reach]
+    along_x(0, (1, nx - 1))
+    for d in (reach, nz - reach):
+        z_copy(d, block_of(0, d), z).wait_recv()
+        if d == reach:
+            for k in range(reach, 0, -1):
+                send(z_copy(reach + k, block_of(0, d), at_z(k)))
+        else:
+            for k in range(reach - 1, 0, -1):
+                send(z_copy(nz - reach - k, block_of(0, d), at_z(nz - k)))
+    for d in near[1:]:
+        if d not in (reach, nz - reach):
+            z_copy(d, block_of(0, d), z).wait_recv()
+        along_x(d, (1, nx - 1))
+    for d in near:
+        e = 1 if d % 2 == 0 else nx - 1
+        x_copy(d, e, block_of(e, d), x).wait_recv()
+        send(x_copy(d, 2, block_of(e, d), at_x(e)))
+    for d in far:
+        z_copy(d, block_of(0, d), z).wait_recv()
+        along_x(d, (1, nx - 1, 2))
+    wo_in.wait()
+    for d in order:
+        passed = 1 if d % 2 == 0 else nx - 1
         for e in range(1, nx):
-            send(remote(ag.at[block], ag.at[block], ax_s.at[d, e], ax_r.at[d, e], {"x": at_x(e)}))
-    wo_in.wait()
-    for d in [0] + by_distance(nz):
-        for e in range(1, nx):
-            src_x = at_x(nx - e)
-            block = src_x * nz + at_z(nz - d)
-            remote(ag.at[block], ag.at[block], ax_s.at[d, e], ax_r.at[d, e], {"x": src_x}).wait_recv()
+            if d in far or e != passed:
+                x_copy(d, e, block_of(e, d), x).wait_recv()
 
     group = 16 // slots
     for g in range(rows // 16):
@@ -386,16 +418,16 @@
     for k in range(att.shape[1] // tile):
         picked = dot(pr[...], att[:, k * tile : (k + 1) * tile]).astype(BF16)
         update = update + dot(picked, wo[k * tile : (k + 1) * tile, :])
-    nst[...] = update.reshape(nn, rows_n, wo.shape[1])
+    total = update.reshape(nn, rows_n, wo.shape[1])
+    mine[...] = total
+    nst[...] = total.astype(BF16)
     for d in range(1, nn):
-        send(remote(nst.at[at_n(d)], nin.at[n], no_s.at[d], no_r.at[d], {"narrow": at_n(d)}))
-    nin[n] = nst[n]
+        send(remote(nst.at[at_n(d)], nin.at[d], no_s.at[d], no_r.at[d], {"narrow": at_n(d)}))
+    result = mine[n]
     for d in range(1, nn):
         src = at_n(nn - d)
-        remote(nst.at[0], nin.at[src], no_s.at[d], no_r.at[d], {"narrow": src}).wait_recv()
-    result = nin[0]
-    for k in range(1, nn):
-        result = result + nin[k]
+        remote(nst.at[0], nin.at[d], no_s.at[d], no_r.at[d], {"narrow": src}).wait_recv()
+        result = result + nin[d].astype(F32)
     out_ref[...] = (nres[n, x].astype(F32) + result).astype(BF16)
 
     for copy in sends:
@@ -456,7 +488,8 @@
         pltpu.VMEM((nx * nz, slots, query_cols), BF16),
         pltpu.VMEM((rows, query_cols), BF16),
         pltpu.VMEM((nn, rows_n, w_out.shape[1]), F32),
-        pltpu.VMEM((nn, rows_n, w_out.shape[1]), F32),
+        pltpu.VMEM((nn, rows_n, w_out.shape[1]), BF16),
+        pltpu.VMEM((nn, rows_n, w_out.shape[1]), BF16),
         dma((7,)),
         dma((nx,)), dma((nx,)), dma((nx,)), dma((nx,)), dma((nx,)), dma((nx,)),
         dma((2,)), dma((2,)),

time: 88.7 us -> 84.9 us (0.957)
  Pallas kernels: 87.1 us -> 83.3 us
    pallas_call x1, Pallas kernels: 87.1 us -> 83.3 us  [per_device(): pl.pallas_call(functools.partial(kernel, nx, nz, nn, width), out_shape=ja...]
where the time goes in v4:
time: 84.9 us; the launch traced here: 84.6 us
  Pallas kernels  83.3 us (98%)
  local copies, waits for them, and re-layouts  1.32 us (2%)
    pallas_call x1, Pallas kernels, per_device(): pl.pallas_call(functools.partial(kernel, nx, nz, nn, width), out_shape=ja...  83.3 us

profile of v4, /device:TPU:1, one launch (start us, length us, event | category | flops | bytes accessed | tf_op | source)
XLA Modules:
  0.0 84.6 jit_solution(8448797350919694410)
XLA Ops:
  0.0 83.3 %decode_block.1 = bf16[32,256]{1,0:T(8,128)(2,1)} custom-call(s32[256]{0:T(256)} %lens.1, s32[256]{0:T(256)} %asg.1, bf16[32,256]{1,0:T(8,128)(2,1)} %res_h.1, bf16[256]{0:T(256)(128)(2,1)} %gain_h.1, s32[1,256]{1,0:T(1,128)} %bitcast.5, bf16[256,2048]{1,0:T(8,128)(2,1)} %wq_h.1, bf16[512,128]{1,0:T(8,128)(2,1)} %bitcast.4, bf16[2048,256]{1,0:T(8,128)(2,1)} %wo_h.1, ...), custom_call_target="tpu_custom_call" | custom-call | tf_op jit(solution)/shard_map/decode_block/pallas_call | solution.py:505
  83.3 1.3 %copy.11 = bf16[32,256]{1,0:T(8,128)(2,1)} copy(bf16[32,256]{1,0:T(8,128)(2,1)} %decode_block.1) | data formatting | bytes 32768

commit v5 on v4

--- a/solution.py
+++ b/solution.py
@@ -258,15 +258,6 @@
     def _():
         remote(kvs.at[0], kvw.at[1], kv_s.at[0], kv_r.at[1], {"x": x // 2}).wait_recv()
 
-    total = dot(nrm[:, :kw], wq[0])
-    for k in range(1, nx):
-        total = total + dot(nrm[:, k * kw : (k + 1) * kw], wq[k])
-    for k in range(pieces - 1):
-        part[:, k] = total[:, k * HD : (k + 1) * HD].reshape(nz, per_z, HD)
-    half = nrm[:, pl.ds(pl.multiple_of(lax.rem(x, 2) * 2 * kw, 2 * kw), 2 * kw)]
-    kv_part = dot(half[:, :kw], kvw[0]) + dot(half[:, kw:], kvw[1])
-    part[:, pieces - 1] = kv_part.reshape(nz, per_z, HD)
-
     steps = nz // 4
     sides = ((1, r_even, r_odd, re_s, re_r, ro_s, ro_r), (-1, l_even, l_odd, le_s, le_r, lo_s, lo_r))
 
@@ -288,14 +279,26 @@
         to = {"z": along(side, 2)}
         return remote(src, side[1].at[s, k], side[3].at[s, k], side[4].at[s, k], to)
 
-    for k in range(pieces):
+    def start_piece(k):
         send(even_copy(sides[0], 0, k))
         for side in sides:
             send(odd_copy(side, steps - 1, k))
-    for i in range(steps - 2, -1, -1):
-        for k in range(pieces):
-            for side in sides:
-                send(odd_copy(side, i, k))
+
+    for k in range(0, pieces - 1, 2):
+        cols = slice(k * HD, (k + 2) * HD)
+        total = dot(nrm[:, :kw], wq[0, :, cols])
+        for t in range(1, nx):
+            total = total + dot(nrm[:, t * kw : (t + 1) * kw], wq[t, :, cols])
+        for h in range(2):
+            part[:, k + h] = total[:, h * HD : (h + 1) * HD].reshape(nz, per_z, HD)
+            start_piece(k + h)
+    half = nrm[:, pl.ds(pl.multiple_of(lax.rem(x, 2) * 2 * kw, 2 * kw), 2 * kw)]
+    kv_part = dot(half[:, :kw], kvw[0]) + dot(half[:, kw:], kvw[1])
+    part[:, pieces - 1] = kv_part.reshape(nz, per_z, HD)
+    start_piece(pieces - 1)
+    for k in range(pieces):
+        for side in sides:
+            send(odd_copy(side, steps - 2, k))
     for s in range(1, steps):
         for k in range(pieces):
             for side in sides:
@@ -307,6 +310,10 @@
                     even_copy(side, s - 1, k).wait_recv()
                     side[1][s - 1, k] = side[1][s - 1, k] + side[2][steps - s, k] + own_part
                 send(even_copy(side, s, k))
+        if s + 1 < steps:
+            for k in range(pieces):
+                for side in sides:
+                    send(odd_copy(side, steps - s - 2, k))
     for k in range(pieces):
         own = part[z, k]
         for side in sides:
@@ -331,12 +338,11 @@
     def rotate(v):
         return (v * cosine + pltpu.roll(v, HD // 2, 1) * sine).astype(BF16).astype(F32)
 
-    for k in range(pieces):
+    for i in range(pieces):
         for d in range(1, nx):
             src = at_x(nx - d)
-            remote(xs.at[0, k], xin.at[src, k], xe_s.at[d, k], xe_r.at[d, k], {"x": src}).wait_recv()
-    for k in range(nx):
-        for i in range(heads_x):
+            remote(xs.at[0, i], xin.at[src, i], xe_s.at[d, i], xe_r.at[d, i], {"x": src}).wait_recv()
+        for k in range(nx if i < heads_x else 0):
             turned_query = rotate(xin[k, i])
             for j in range(slots):
                 q_ref[j, k * heads_x + i : k * heads_x + i + 1, :] = turned_query[j : j + 1]

time: 84.9 us -> 83.7 us (0.986)
  Pallas kernels: 83.3 us -> 82.1 us
    pallas_call x1, Pallas kernels: 83.3 us -> 82.1 us  [per_device(): pl.pallas_call(functools.partial(kernel, nx, nz, nn, width), out_shape=ja...]
where the time goes in v5:
time: 83.7 us; the launch traced here: 83.5 us
  Pallas kernels  82.1 us (98%)
  local copies, waits for them, and re-layouts  1.32 us (2%)
    pallas_call x1, Pallas kernels, per_device(): pl.pallas_call(functools.partial(kernel, nx, nz, nn, width), out_shape=ja...  82.1 us

profile of v5, /device:TPU:1, one launch (start us, length us, event | category | flops | bytes accessed | tf_op | source)
XLA Modules:
  0.0 83.5 jit_solution(1932380646775104422)
XLA Ops:
  0.0 82.1 %decode_block.1 = bf16[32,256]{1,0:T(8,128)(2,1)} custom-call(s32[256]{0:T(256)} %lens.1, s32[256]{0:T(256)} %asg.1, bf16[32,256]{1,0:T(8,128)(2,1)} %res_h.1, bf16[256]{0:T(256)(128)(2,1)} %gain_h.1, s32[1,256]{1,0:T(1,128)} %bitcast.5, bf16[256,2048]{1,0:T(8,128)(2,1)} %wq_h.1, bf16[512,128]{1,0:T(8,128)(2,1)} %bitcast.4, bf16[2048,256]{1,0:T(8,128)(2,1)} %wo_h.1, ...), custom_call_target="tpu_custom_call" | custom-call | tf_op jit(solution)/shard_map/decode_block/pallas_call | solution.py:511
  82.2 1.3 %copy.11 = bf16[32,256]{1,0:T(8,128)(2,1)} copy(bf16[32,256]{1,0:T(8,128)(2,1)} %decode_block.1) | data formatting | bytes 32768

commit v6 on v5

--- a/solution.py
+++ b/solution.py
@@ -43,7 +43,7 @@
     lens, asg, res_h, gain_h, asg_ref, wq_h, wkv_h, wo_h, cache_h, tab_h,
     out_ref,
     nres, gains, wq, wkv, kvs, kvw, wo, cache, kc, vc, tab,
-    gain_v, zin, nsq, pz, pr, sres, nrm, part, r_even, r_odd, l_even, l_odd, wrel, xs, xin, q_ref, ab, ag, att, mine, nst, nin,
+    gain_v, zin, nsq, pz, pr, sres, nrm, part, r_even, r_odd, l_even, l_odd, wrel, xs, xin, q_ref, ab, ag, att, nst, nin,
     loc, xr_s, xr_r, xg_s, xg_r, xw_s, xw_r, kv_s, kv_r, ng_s, ng_r,
     zs_s, zs_r, ns_s, ns_r, re_s, re_r, ro_s, ro_r, le_s, le_r, lo_s, lo_r, wr_s, wr_r, wf_s, wf_r, xe_s, xe_r,
     az_s, az_r, ax_s, ax_r, no_s, no_r,
@@ -81,6 +81,7 @@
     def wq_part(t):
         return wq_h.at[:, pl.ds(pl.multiple_of(t * qcols, qcols), qcols)]
 
+    far_first = sorted(range(1, nn), key=lambda d: -min(d // 2, (nn - d) // 2))
     local = [
         pltpu.make_async_copy(gain_h, gain_v, loc.at[6]),
         pltpu.make_async_copy(wkv_h, wkv, loc.at[0]),
@@ -91,7 +92,9 @@
         pltpu.make_async_copy(tab_h, tab, loc.at[5]),
     ]
     barrier = pltpu.get_barrier_semaphore()
-    for d in reversed(by_distance(nz)):
+    reach = nz // 4
+    z_near = [d for d in by_distance(nz) if min(d, nz - d) <= reach]
+    for d in reversed(z_near):
         pl.semaphore_signal(barrier, inc=1, device_id={"z": at_z(d)}, device_id_type=MESH)
     for d in range(1, nx):
         pl.semaphore_signal(barrier, inc=1, device_id={"x": at_x(d)}, device_id_type=MESH)
@@ -100,7 +103,7 @@
     for copy in local:
         copy.start()
     gain_in, wkv_in, res_in, wq_in, cache_in, wo_in, tab_in = local
-    pl.semaphore_wait(barrier, (nx - 1) + (nz - 1) + (nn - 1))
+    pl.semaphore_wait(barrier, (nx - 1) + len(z_near) + (nn - 1))
 
     sends = []
 
@@ -115,7 +118,7 @@
         half = wq.at[owner, i * (kw // 2) : (i + 1) * (kw // 2)]
         return remote(wrel.at[i], half, wf_s.at[i], wf_r.at[i], {"x": to})
 
-    for d in range(1, nx):
+    for d in (2, 1, nx - 1):
         send(remote(res_h, nres.at[n, x], xr_s.at[d], xr_r.at[d], {"x": at_x(d)}))
     gain_in.wait()
     gains[x] = gain_v[...].astype(F32).reshape(1, kw)
@@ -190,8 +193,12 @@
     r_sub = lax.broadcasted_iota(jnp.int32, (rows_n, rows), 0)
     r_lane = lax.broadcasted_iota(jnp.int32, (rows_n, rows), 1)
     zin[z] = jnp.sum(jnp.where(r_lane == r_sub + n * rows_n, squares, 0.0), axis=0, keepdims=True)
-    for d in reversed(by_distance(nz)):
-        send(remote(zin.at[z], zin.at[z], zs_s.at[d], zs_r.at[d], {"z": at_z(d)}))
+
+    def sum_copy(d, src, to):
+        return remote(zin.at[src], zin.at[src], zs_s.at[d], zs_r.at[d], {"z": to})
+
+    for d in reversed(z_near):
+        send(sum_copy(d, z, at_z(d)))
 
     cache_in.wait()
     step = kw
@@ -201,6 +208,15 @@
             kc[j, b * step : (b + 1) * step, :] = dot(e0, block).astype(BF16)
             vc[j, b * step : (b + 1) * step, :] = dot(e1, block).astype(BF16)
 
+    src = at_z(nz - reach)
+    sum_copy(reach, src, z).wait_recv()
+    for k in range(reach, 0, -1):
+        send(sum_copy(reach + k, src, at_z(k)))
+    src = at_z(reach)
+    sum_copy(nz - reach, src, z).wait_recv()
+    for k in range(reach - 1, 0, -1):
+        send(sum_copy(nz - reach - k, src, at_z(nz - k)))
+
     left_x, right_x, opposite = at_x(nx - 1), at_x(1), at_x(2)
     relay_half(0, wrel.at[0], left_x).wait_recv()
     send(relayed(0, left_x, right_x))
@@ -216,10 +232,12 @@
     send(row_copy(6, across, other))
 
     for d in range(1, nz):
+        if d in (reach, nz - reach):
+            continue
         src = at_z(nz - d)
         remote(zin.at[src], zin.at[src], zs_s.at[d], zs_r.at[d], {"z": src}).wait_recv()
     nsq[n] = jnp.sum(zin[...], axis=0)
-    for d in range(1, nn):
+    for d in far_first:
         send(remote(nsq.at[n], nsq.at[n], ns_s.at[d], ns_r.at[d], {"narrow": at_n(d)}))
 
     far = narrow(-2 * turn, 1 - c)
@@ -322,7 +340,7 @@
             own = own + side[1][steps - 1, k] + side[2][0, k]
         for t in range(nx):
             xs[t, k] = own[t * slots : (t + 1) * slots]
-        for d in range(1, nx):
+        for d in (2, 1, nx - 1):
             to = at_x(d)
             send(remote(xs.at[to, k], xin.at[x, k], xe_s.at[d, k], xe_r.at[d, k], {"x": to}))
     xin[x] = xs[x]
@@ -366,8 +384,6 @@
         for h in range(heads):
             ab[j : j + 1, h * HD : (h + 1) * HD] = attended[h : h + 1]
     ag[w_own] = ab[...].astype(BF16)
-
-    reach = nz // 4
 
     def z_copy(d, block, to):
         return remote(ag.at[block], ag.at[block], az_s.at[d], az_r.at[d], {"z": to})
@@ -422,14 +438,16 @@
     tile = 512
     update = jnp.zeros((rows, wo.shape[1]), F32)
     for k in range(att.shape[1] // tile):
-        picked = dot(pr[...], att[:, k * tile : (k + 1) * tile]).astype(BF16)
-        update = update + dot(picked, wo[k * tile : (k + 1) * tile, :])
-    total = update.reshape(nn, rows_n, wo.shape[1])
-    mine[...] = total
-    nst[...] = total.astype(BF16)
-    for d in range(1, nn):
+        cols = slice(k * tile, (k + 1) * tile)
+        update = update + dot(att[:, cols], wo[cols, :])
+    rounded = update.astype(BF16)
+    rest = (update - rounded.astype(F32)).astype(BF16)
+    picked = dot(pr[...], rounded)
+    nst[...] = picked.astype(BF16).reshape(nn, rows_n, wo.shape[1])
+    for d in far_first:
         send(remote(nst.at[at_n(d)], nin.at[d], no_s.at[d], no_r.at[d], {"narrow": at_n(d)}))
-    result = mine[n]
+    own_pick = pr[pl.ds(pl.multiple_of(n * rows_n, rows_n), rows_n), :]
+    result = nst[n].astype(F32) + dot(own_pick, rest)
     for d in range(1, nn):
         src = at_n(nn - d)
         remote(nst.at[0], nin.at[d], no_s.at[d], no_r.at[d], {"narrow": src}).wait_recv()
@@ -493,7 +511,6 @@
         pltpu.VMEM((slots, query_cols), F32),
         pltpu.VMEM((nx * nz, slots, query_cols), BF16),
         pltpu.VMEM((rows, query_cols), BF16),
-        pltpu.VMEM((nn, rows_n, w_out.shape[1]), F32),
         pltpu.VMEM((nn, rows_n, w_out.shape[1]), BF16),
         pltpu.VMEM((nn, rows_n, w_out.shape[1]), BF16),
         dma((7,)),

time: 83.7 us -> 82.8 us (0.989)
  Pallas kernels: 82.1 us -> 81.2 us
    pallas_call x1, Pallas kernels: 82.1 us -> 81.2 us  [per_device(): pl.pallas_call(functools.partial(kernel, nx, nz, nn, width), out_shape=ja...]
where the time goes in v6:
time: 82.8 us; the launch traced here: 82.6 us
  Pallas kernels  81.2 us (98%)
  local copies, waits for them, and re-layouts  1.32 us (2%)
    pallas_call x1, Pallas kernels, per_device(): pl.pallas_call(functools.partial(kernel, nx, nz, nn, width), out_shape=ja...  81.2 us

profile of v6, /device:TPU:1, one launch (start us, length us, event | category | flops | bytes accessed | tf_op | source)
XLA Modules:
  0.0 82.6 jit_solution(15756184278132226644)
XLA Ops:
  0.0 81.2 %decode_block.1 = bf16[32,256]{1,0:T(8,128)(2,1)} custom-call(s32[256]{0:T(256)} %lens.1, s32[256]{0:T(256)} %asg.1, bf16[32,256]{1,0:T(8,128)(2,1)} %res_h.1, bf16[256]{0:T(256)(128)(2,1)} %gain_h.1, s32[1,256]{1,0:T(1,128)} %bitcast.5, bf16[256,2048]{1,0:T(8,128)(2,1)} %wq_h.1, bf16[512,128]{1,0:T(8,128)(2,1)} %bitcast.4, bf16[2048,256]{1,0:T(8,128)(2,1)} %wo_h.1, ...), custom_call_target="tpu_custom_call" | custom-call | tf_op jit(solution)/shard_map/decode_block/pallas_call | solution.py:528
  81.2 1.3 %copy.11 = bf16[32,256]{1,0:T(8,128)(2,1)} copy(bf16[32,256]{1,0:T(8,128)(2,1)} %decode_block.1) | data formatting | bytes 32768

commit v7 on v6

--- a/solution.py
+++ b/solution.py
@@ -423,7 +423,7 @@
         send(x_copy(d, 2, block_of(e, d), at_x(e)))
     for d in far:
         z_copy(d, block_of(0, d), z).wait_recv()
-        along_x(d, (1, nx - 1, 2))
+        along_x(d, (2, 1, nx - 1))
     wo_in.wait()
     for d in order:
         passed = 1 if d % 2 == 0 else nx - 1

time: 82.8 us -> 82.6 us (level)
  no operation moved by 1% of the time
where the time goes in v7:
time: 82.6 us; the launch traced here: 82.4 us
  Pallas kernels  81 us (98%)
  local copies, waits for them, and re-layouts  1.32 us (2%)
    pallas_call x1, Pallas kernels, per_device(): pl.pallas_call(functools.partial(kernel, nx, nz, nn, width), out_shape=ja...  81 us

profile of v7, /device:TPU:1, one launch (start us, length us, event | category | flops | bytes accessed | tf_op | source)
XLA Modules:
  0.0 82.4 jit_solution(6084221652814999563)
XLA Ops:
  0.0 81.0 %decode_block.1 = bf16[32,256]{1,0:T(8,128)(2,1)} custom-call(s32[256]{0:T(256)} %lens.1, s32[256]{0:T(256)} %asg.1, bf16[32,256]{1,0:T(8,128)(2,1)} %res_h.1, bf16[256]{0:T(256)(128)(2,1)} %gain_h.1, s32[1,256]{1,0:T(1,128)} %bitcast.5, bf16[256,2048]{1,0:T(8,128)(2,1)} %wq_h.1, bf16[512,128]{1,0:T(8,128)(2,1)} %bitcast.4, bf16[2048,256]{1,0:T(8,128)(2,1)} %wo_h.1, ...), custom_call_target="tpu_custom_call" | custom-call | tf_op jit(solution)/shard_map/decode_block/pallas_call | solution.py:528
  81.1 1.3 %copy.11 = bf16[32,256]{1,0:T(8,128)(2,1)} copy(bf16[32,256]{1,0:T(8,128)(2,1)} %decode_block.1) | data formatting | bytes 32768
